TPU v7x, 32 devices: a whole 2x2x4 slice. The times are simulated.
32 devices in a mesh: fx: 4 (over y, x), fy: 8 (over z, core).
Axes of the slice: x: 2, y: 2, z: 4, core: 2. Of those that a mesh axis runs over, the one named last changes fastest.
Arguments:
- sky: bfloat16 [4096, 32768], P('fx', 'fy'), may hold values from -6 to 6
- sub_off: int32 [2, 4], replicated, may hold values from 0 to 32767
- readers: int32 [32], replicated, may hold values from 0 to 3, as said below
- vis_cells: int32 [2, 65536], P(None, ('fx', 'fy')), may hold values from 0 to 504
- row_kernel: bfloat16 [8, 65536], P(None, ('fx', 'fy')), may hold values from 0.049804688 to 1
- col_kernel: float32 [8, 65536], P(None, ('fx', 'fy')), may hold values from 0.05 to 1
Outputs:
- vis: float32 [2, 65536], P(None, ('fx', 'fy'))
Inputs may be any that keep to these rules, and one draw needn't show every extreme that they name: `readers`: every subgrid is read by at least one reader.
All inputs are finite; a program needn't handle non-finite values.
Results may differ from a plain program's by a relative error of at most 0.0064.
Values may be sent and summed in bfloat16 or wider, within the bound.
No kernel may reach another device: no remote copies, remote signals or barrier semaphores. Data moves between devices by JAX's collectives and lax.ppermute only.
A program may use at most 128 MiB of HBM per device.

v0:
```python
import functools
import math

import jax
import jax.numpy as jnp
from jax import lax
from jax.experimental import pallas as pl
from jax.experimental.pallas import tpu as pltpu
from jax.sharding import PartitionSpec as P


FACET = 4096
SUB = 512
K = 128
FR = 512
NSUB = 4
W = 8
STEP = 64
GROUP = 8
VBLOCK = 256
HALF = SUB // 2
F32 = jnp.float32
BF16 = jnp.bfloat16
SMEM = pl.BlockSpec(memory_space=pltpu.SMEM)
VMEM = pl.BlockSpec(memory_space=pltpu.VMEM)
ANY = pl.BlockSpec(memory_space=pl.ANY)


def wave(turns, period):
    bits = period.bit_length() - 1
    phase = turns & (period - 1)
    quarter = (phase + period // 8) >> (bits - 2)
    theta = (phase - (quarter << (bits - 2))).astype(F32) * (2.0 * math.pi / period)
    square = theta * theta
    sine = theta * (
        1.0
        + square
        * (-1.0 / 6 + square * (1.0 / 120 + square * (-1.0 / 5040 + square * (1.0 / 362880))))
    )
    cosine = 1.0 + square * (
        -0.5
        + square
        * (1.0 / 24 + square * (-1.0 / 720 + square * (1.0 / 40320 - square * (1.0 / 3628800))))
    )
    odd = (quarter & 1) == 1
    real_part = jnp.where(odd, sine, cosine)
    imag_part = jnp.where(odd, cosine, sine)
    real_part = jnp.where(((quarter + 1) & 2) == 2, -real_part, real_part)
    imag_part = jnp.where((quarter & 2) == 2, -imag_part, imag_part)
    return real_part, imag_part


def turn(first, second, sky_cells, scale=1.0):
    real_part, imag_part = wave(first * second, sky_cells)
    return real_part * scale, imag_part * -scale


def amplitude(gap):
    top = wave(gap, 2 * SUB // K)[1]
    below = wave(gap, 2 * SUB)[1]
    return jnp.where(gap == 0, 1.0, top / (K * jnp.where(gap == 0, 1.0, below)))


def middle_of(start, sky_cells):
    return start + (K - 1) * (sky_cells // (2 * SUB))


def iota(shape, dimension):
    return lax.broadcasted_iota(jnp.int32, shape, dimension)


def expand(coarse_real, coarse_imag, fine_real, fine_imag):
    return (
        coarse_real * fine_real - coarse_imag * fine_imag,
        coarse_real * fine_imag + coarse_imag * fine_real,
    )


def parts_of(index):
    return slice(2 * index * K, (2 * index + 1) * K), slice((2 * index + 1) * K, (2 * index + 2) * K)


def tables_kernel(steps, geometry, meta, out_cols, out_rows, coarse_col, fine_col):
    sky_cells, row_spacing, copies = geometry
    count, columns = len(steps), out_cols.shape[1]
    facets = out_rows.shape[0] // count
    at_x, at_y = meta[0], meta[1]
    own = at_y // 2 // copies
    lane, row = iota((STEP, K), 1), iota((STEP, K), 0)
    re, im = parts_of(0)
    for s, step in enumerate(steps):
        chosen = (own + step) % NSUB
        pair, (out_re, out_im) = s // 2, parts_of(s % 2)
        frequency = meta[2 + NSUB + chosen] + SUB // K * lane
        coarse_col[s, :, re], coarse_col[s, :, im] = turn(
            frequency, at_y * FACET + STEP * row, sky_cells, 1.0 / math.sqrt(FACET)
        )
        fine_col[:, re], fine_col[:, im] = turn(frequency, row, sky_cells)

        def table_turn(group, carry):
            coarse = coarse_col[s, pl.ds(pl.multiple_of(group * GROUP, GROUP), GROUP), :]
            for piece in range(GROUP):
                here = pl.ds(pl.multiple_of((group * GROUP + piece) * STEP, STEP), STEP)
                real_part, imag_part = expand(
                    coarse[piece : piece + 1, re],
                    coarse[piece : piece + 1, im],
                    fine_col[:, re],
                    fine_col[:, im],
                )
                out_cols[pair, here, out_re] = real_part.astype(BF16)
                out_cols[pair, here, out_im] = imag_part.astype(BF16)
            return carry

        lax.fori_loop(0, columns // (STEP * GROUP), table_turn, 0)
        frequency = meta[2 + chosen] + SUB // K * lane
        fine_real, fine_imag = turn(frequency, row, sky_cells)
        pieces = FR // STEP
        for a in range(facets):
            row_start = (at_x * facets + a) * row_spacing
            coarse_real, coarse_imag = turn(
                frequency[:pieces], row_start + STEP * row[:pieces], sky_cells, 1.0 / math.sqrt(FR)
            )
            for piece in range(pieces):
                here = slice(piece * STEP, (piece + 1) * STEP)
                real_part, imag_part = expand(
                    coarse_real[piece : piece + 1],
                    coarse_imag[piece : piece + 1],
                    fine_real,
                    fine_imag,
                )
                out_rows[s * facets + a, here, re] = real_part.astype(BF16)
                out_rows[s * facets + a, here, im] = imag_part.astype(BF16)


def strip_tables(meta, sky, steps, geometry):
    count, (rows, columns) = len(steps), sky.shape
    facets = rows // FR
    return pl.pallas_call(
        functools.partial(tables_kernel, steps, geometry),
        in_specs=[SMEM],
        out_specs=[VMEM] * 2,
        out_shape=[
            jax.ShapeDtypeStruct((count // 2, columns, 4 * K), BF16),
            jax.ShapeDtypeStruct((count * facets, FR, 2 * K), BF16),
        ],
        scratch_shapes=[
            pltpu.VMEM((count, columns // STEP, 2 * K), F32),
            pltpu.VMEM((STEP, 2 * K), F32),
        ],
        cost_estimate=pl.CostEstimate(flops=1 << 33, bytes_accessed=1 << 24, transcendentals=0),
        compiler_params=pltpu.CompilerParams(vmem_limit_bytes=16 << 20),
        name="strip_tables",
    )(meta)


def blocks_kernel(pair, sky, cols, rows, *outs):
    facets = sky.shape[0] // FR
    for a in range(facets):
        strips = jnp.dot(
            sky[a * FR : (a + 1) * FR, :], cols[pair], preferred_element_type=F32
        ).astype(BF16)
        for s in range(2):
            product = lax.dot_general(
                strips[:, 2 * s * K : (2 * s + 2) * K],
                rows[(2 * pair + s) * facets + a],
                (((0,), (0,)), ((), ())),
                preferred_element_type=F32,
            )
            re, im = parts_of(a)
            outs[s][:, re] = (product[:K, :K] - product[K:, K:]).astype(BF16)
            outs[s][:, im] = (product[:K, K:] + product[K:, :K]).astype(BF16)


def facet_blocks(sky, tables, pair):
    rows, columns = sky.shape
    facets = rows // FR
    return pl.pallas_call(
        functools.partial(blocks_kernel, pair),
        in_specs=[VMEM] * 3,
        out_specs=[VMEM] * 2,
        out_shape=[jax.ShapeDtypeStruct((K, 2 * facets * K), BF16)] * 2,
        cost_estimate=pl.CostEstimate(
            flops=8 * rows * columns * K, bytes_accessed=2 * rows * columns, transcendentals=0
        ),
        compiler_params=pltpu.CompilerParams(vmem_limit_bytes=28 << 20),
        name="facet_blocks",
    )(sky, *tables)


def col_table_kernel(geometry, factor, place, after, out):
    sky_cells, copies, sources = geometry
    planes = len(sources) * copies
    period = 2 * planes
    at_y = place[1]
    plane, core = at_y // 2, at_y % 2
    own = plane // copies
    gap = core * HALF + iota((HALF, K), 0) - SUB // K * iota((HALF, K), 1)
    size = amplitude(gap) * factor
    real_part, imag_part = wave(gap * middle_of(0, sky_cells), sky_cells)
    folded = (HALF // period, period, K)
    real_part = (size * real_part).reshape(folded)
    imag_part = (size * imag_part).reshape(folded)
    steps = gap[:period]
    at = 0
    for other in range(2):
        for step in sources:
            for copy_step in range(copies):
                source = (own + NSUB - step) % NSUB * copies + (plane + copies - copy_step) % copies
                turned = wave(steps * (2 * source + (core + other) % 2), period)
                both = expand(real_part, imag_part, turned[0][None], turned[1][None])
                out[at, :HALF, :] = both[0].reshape(HALF, K).astype(BF16)
                out[at, HALF:, :] = both[1].reshape(HALF, K).astype(BF16)
                at += 1


def row_table_kernel(geometry, place, after, out):
    sky_cells, facets, rows_axis = geometry
    period = facets * rows_axis
    gap = iota((K, SUB), 1) - SUB // K * iota((K, SUB), 0)
    size = amplitude(gap)
    real_part, imag_part = wave(gap * middle_of(0, sky_cells), sky_cells)
    folded = (K // period, period, SUB)
    real_part = (size * real_part).reshape(folded)
    imag_part = (size * imag_part).reshape(folded)
    steps = gap[:period]
    for source in range(period):
        step, a = source // facets, source % facets
        facet_row = (place[0] + rows_axis - step) % rows_axis * facets + a
        turned = wave(steps * facet_row, period)
        both = expand(real_part, imag_part, turned[0][None], turned[1][None])
        out[source, :, :SUB] = both[0].reshape(K, SUB).astype(BF16)
        out[source, :, SUB:] = both[1].reshape(K, SUB).astype(BF16)


def columns_kernel(count, facets, table, *refs):
    blocks, out = refs[:count], refs[count]
    total = None
    for pair in range(0, count, 2):
        stacked = jnp.concatenate([block[...] for block in blocks[pair : pair + 2]], axis=0)
        turned = jnp.concatenate([table[at] for at in range(pair, min(pair + 2, count))], axis=1)
        part = jnp.dot(turned, stacked, preferred_element_type=F32)
        total = part if total is None else total + part
    for a in range(facets):
        re, im = parts_of(a)
        out[:HALF, a * K : (a + 1) * K] = (total[:HALF, re] - total[HALF:, im]).astype(BF16)
        out[HALF:, a * K : (a + 1) * K] = (total[:HALF, im] + total[HALF:, re]).astype(BF16)


def column_sums(table, blocks):
    facets = blocks[0].shape[1] // (2 * K)
    return pl.pallas_call(
        functools.partial(columns_kernel, len(blocks), facets),
        out_shape=jax.ShapeDtypeStruct((2 * HALF, facets * K), BF16),
        cost_estimate=pl.CostEstimate(
            flops=8 * HALF * len(blocks) * facets * K * K, bytes_accessed=1 << 21, transcendentals=0
        ),
        compiler_params=pltpu.CompilerParams(vmem_limit_bytes=20 << 20),
        name="column_sums",
    )(table, *blocks)


def taps_of(first, kernel, shape):
    row = iota(shape, 0)
    tap = (row - first) & (W - 1)
    value = jnp.zeros(shape, F32)
    for e in range(W):
        value = jnp.where(tap == e, kernel[e : e + 1, :], value)
    return value, (first - row + (W - 1)) >> 3


def query_kernel(vis_cells, row_kernel, col_kernel, after, out):
    out[0:W, :] = row_kernel[...]
    out[W : 2 * W, :] = col_kernel[...].astype(BF16)
    cells = vis_cells[...]
    halves = [cells >> 1, cells & 1]
    cells = jnp.concatenate([half[axis : axis + 1] for axis in range(2) for half in halves])
    out[2 * W :, :] = cells.astype(F32).astype(BF16)


def degrid_kernel(geometry, place, readers, table, queries_own, queries_other, *refs):
    cols_axis, copies, count = geometry
    sums, outs, subgrid = refs[:count], refs[count : count + 2], refs[count + 2]
    at_x, at_y = place[0], place[1]
    plane, core = at_y // 2, at_y % 2
    own = plane // copies
    total = None
    facets = sums[0].shape[1] // K
    for source in range(count):
        turned = jnp.concatenate(
            [table[at] for at in range(source * facets, (source + 1) * facets)], axis=0
        )
        part = jnp.dot(sums[source][...], turned, preferred_element_type=F32)
        total = part if total is None else total + part
    subgrid[:HALF, :] = (total[:HALF, :SUB] - total[HALF:, SUB:]).astype(BF16)
    subgrid[HALF:, :] = (total[:HALF, SUB:] + total[HALF:, :SUB]).astype(BF16)
    planes, _, visibilities = queries_own.shape
    for other, (queries, out) in enumerate(zip((queries_own, queries_other), outs)):

        def slot_turn(slot, carry):
            source = (plane + planes - slot) % planes
            reader = at_x * cols_axis + 2 * source + (core + other) % 2
            active = (readers[reader] == own) & (source % copies == plane % copies)

            @pl.when(jnp.logical_not(active))
            def _():
                out[slot] = jnp.zeros(out.shape[1:], F32)

            @pl.when(active)
            def _():
                def block_turn(block, carry):
                    here = pl.ds(pl.multiple_of(block * VBLOCK, VBLOCK), VBLOCK)
                    rows = queries[slot, :, here].astype(F32)
                    u = (rows[16:17] * 2.0 + rows[17:18]).astype(jnp.int32)
                    w = (rows[18:19] * 2.0 + rows[19:20]).astype(jnp.int32)
                    row_value, row_group = taps_of(u, rows[0:8], (W, VBLOCK))
                    groups = iota((SUB // W, W, VBLOCK), 0)
                    weights = jnp.where(groups == row_group[None], row_value[None], 0.0)
                    weights = weights.reshape(SUB, VBLOCK).astype(BF16)
                    spread = jnp.dot(subgrid[...], weights, preferred_element_type=F32)
                    spread = spread.reshape(2, HALF // W, W, VBLOCK)
                    col_value, col_group = taps_of(w, rows[8:16], (W, VBLOCK))
                    groups = iota((HALF // W, W, VBLOCK), 0)
                    hit = groups == (col_group - core * (HALF // W))[None]
                    for p in range(2):
                        picked = jnp.sum(jnp.where(hit, spread[p], 0.0), axis=0)
                        out[slot, p : p + 1, here] = jnp.sum(
                            picked * col_value, axis=0, keepdims=True
                        )
                    return carry

                lax.fori_loop(0, visibilities // VBLOCK, block_turn, 0)

            return carry

        lax.fori_loop(0, planes, slot_turn, 0)


def degrid(place, readers, table, queries, others, sums, geometry):
    planes, _, visibilities = queries.shape
    result = jax.ShapeDtypeStruct((planes, 2, visibilities), F32)
    return pl.pallas_call(
        functools.partial(degrid_kernel, geometry + (len(sums),)),
        in_specs=[SMEM, SMEM] + [VMEM] * (3 + len(sums)),
        out_specs=[VMEM, VMEM],
        out_shape=[result, result],
        scratch_shapes=[pltpu.VMEM((2 * HALF, SUB), BF16)],
        cost_estimate=pl.CostEstimate(flops=1 << 33, bytes_accessed=1 << 22, transcendentals=0),
        compiler_params=pltpu.CompilerParams(vmem_limit_bytes=20 << 20),
        name="degrid",
    )(place, readers, table, queries, others, *sums)


def local(sky, sub_off, readers, vis_cells, row_kernel, col_kernel):
    rows_axis = lax.axis_size("fx")
    cols_axis = lax.axis_size("fy")
    planes = cols_axis // 2
    copies = planes // NSUB
    facets = sky.shape[0] // FR
    sky_cells = FACET * cols_axis
    facet_rows = facets * rows_axis
    row_spacing = sky_cells // facet_rows
    factor = 1.0 / math.sqrt(facet_rows * cols_axis)
    assert planes == copies * NSUB and sky_cells & (sky_cells - 1) == 0
    place = jnp.stack([lax.axis_index("fx"), lax.axis_index("fy")]).astype(jnp.int32)
    meta = jnp.concatenate([place, sub_off.reshape(-1)])

    def plane_shift(group_step, copy_step):
        moved = []
        for z in range(planes):
            to = (z // copies + group_step) % NSUB * copies + (z % copies + copy_step) % copies
            moved += [(2 * z + c, 2 * to + c) for c in range(2)]
        return moved

    swap = [(i, i ^ 1) for i in range(cols_axis)]

    steps = sorted(range(1, NSUB), key=lambda step: -min(step, NSUB - step)) + [0]
    tables = strip_tables(meta, sky, steps, (sky_cells, row_spacing, copies))
    blocks = []
    for start in range(0, NSUB, 2):
        pair = facet_blocks(sky, tables, start // 2)
        for step, block in zip(steps[start : start + 2], pair):
            for copy_step in range(copies):
                moved = block
                if step or copy_step:
                    moved = lax.ppermute(block, "fy", plane_shift(step, copy_step))
                blocks.append(moved)
    col_table = pl.pallas_call(
        functools.partial(col_table_kernel, (sky_cells, copies, steps), factor),
        in_specs=[SMEM, ANY],
        out_specs=VMEM,
        out_shape=jax.ShapeDtypeStruct((2 * len(blocks), 2 * HALF, K), BF16),
        cost_estimate=pl.CostEstimate(flops=1 << 22, bytes_accessed=1 << 20, transcendentals=1 << 20),
        compiler_params=pltpu.CompilerParams(vmem_limit_bytes=20 << 20),
        name="col_table",
    )(place, pair[0])
    query = pl.pallas_call(
        query_kernel,
        in_specs=[VMEM, VMEM, VMEM, ANY],
        out_specs=VMEM,
        out_shape=jax.ShapeDtypeStruct((2 * W + 4, vis_cells.shape[1]), BF16),
        compiler_params=pltpu.CompilerParams(vmem_limit_bytes=20 << 20),
        name="query",
    )(vis_cells, row_kernel, col_kernel, pair[0])
    last = len(blocks) - copies - 1
    blocks[last], _ = lax.optimization_barrier((blocks[last], col_table))
    blocks += [lax.ppermute(block, "fy", swap) for block in blocks]
    sums = [column_sums(col_table, blocks)]

    for step in range(1, rows_axis):
        ring = [(i, (i + step) % rows_axis) for i in range(rows_axis)]
        sums.append(lax.ppermute(sums[0], "fx", ring))
    row_table = pl.pallas_call(
        functools.partial(row_table_kernel, (sky_cells, facets, rows_axis)),
        in_specs=[SMEM, ANY],
        out_specs=VMEM,
        out_shape=jax.ShapeDtypeStruct((facet_rows, K, 2 * SUB), BF16),
        cost_estimate=pl.CostEstimate(
            flops=1 << 23, bytes_accessed=1 << 21, transcendentals=1 << 21
        ),
        compiler_params=pltpu.CompilerParams(vmem_limit_bytes=20 << 20),
        name="row_table",
    )(place, sums[0])

    moved, _ = lax.optimization_barrier((query, sums[0]))
    queries = [query]
    for step in range(1, planes):
        ring = [(i, (i + 2 * step) % cols_axis) for i in range(cols_axis)]
        queries.append(lax.ppermute(moved, "fy", ring))
    queries = jnp.stack(queries)
    others = lax.ppermute(queries, "fy", swap)
    results, others = degrid(
        place, readers, row_table, queries, others, sums, (cols_axis, copies)
    )

    both = results + lax.ppermute(others, "fy", swap)
    vis = both[0]
    for step in range(1, planes):
        ring = [(i, (i - 2 * step) % cols_axis) for i in range(cols_axis)]
        vis = vis + lax.ppermute(both[step], "fy", ring)
    return vis


def solution(mesh):
    return jax.shard_map(
        local,
        mesh=mesh,
        in_specs=(
            P("fx", "fy"),
            P(),
            P(),
            P(None, ("fx", "fy")),
            P(None, ("fx", "fy")),
            P(None, ("fx", "fy")),
        ),
        out_specs=P(None, ("fx", "fy")),
        check_vma=False,
    )
```

profile of v0, /device:TPU:0, one launch (start us, length us, event | category | flops | bytes accessed | tf_op | source)
XLA Modules:
  0.0 84.1 jit_solution(2183810162500927496)
XLA Ops:
  0.0 0.8 reshape.3
  0.8 0.1 pad_add_fusion.1.meta
  0.8 0.0 copy-start
  0.8 4.7 %strip_tables.1 = (bf16[2,4096,512]{2,1,0:T(8,128)(2,1)S(1)}, bf16[8,512,256]{2,1,0:T(8,128)(2,1)S(1)}) custom-call(s32[10]{0:T(128)S(1)} %pad_add_fusion.1.meta), custom_call_target="tpu_custom_call" | custom-call | flops 8589934592 | bytes 16777216 | tf_op jit(solution)/shard_map/strip_tables/pallas_call | solution.py:138
  5.6 0.0 copy-done
  5.6 5.0 %facet_blocks.2 = (bf16[128,512]{1,0:T(8,128)(2,1)S(1)}, bf16[128,512]{1,0:T(8,128)(2,1)S(1)}) custom-call(bf16[1024,4096]{1,0:T(8,128)(2,1)S(1)} %copy-done, bf16[2,4096,512]{2,1,0:T(8,128)(2,1)S(1)} %get-tuple-element.15.cols, bf16[8,512,256]{2,1,0:T(8,128)(2,1)S(1)} %get-tuple-element.16.rows), custom_call_target="tpu_custom_call" | custom-call | flops 4294967296 | bytes 8388608 | tf_op jit(solution)/shard_map/facet_blocks/pallas_call | solution.py:177
  10.6 0.0 copy-start.1
  10.6 0.0 copy-start.2
  10.6 0.0 copy-start.3
  10.6 5.1 %collective-permute-start.2 = (bf16[128,512]{1,0:T(8,128)(2,1)S(1)}, bf16[128,512]{1,0:T(8,128)(2,1)S(1)}, u32[]{:S(2)}, u32[]{:S(2)}) collective-permute-start(bf16[128,512]{1,0:T(8,128)(2,1)S(1)} %get-tuple-element.17.after), channel_id=1, source_target_pairs={{0,6},{1,7},{2,0},{3,1},{4,2},{5,3},{6,4},{7,5},{8,14},{9,15},{10,... | collective-permute-start | bytes 393224 | tf_op jit(solution)/shard_map/ppermute | solution.py:385
  15.8 5.0 %facet_blocks.3 = (bf16[128,512]{1,0:T(8,128)(2,1)S(1)}, bf16[128,512]{1,0:T(8,128)(2,1)S(1)}) custom-call(bf16[1024,4096]{1,0:T(8,128)(2,1)S(1)} %copy-done, bf16[2,4096,512]{2,1,0:T(8,128)(2,1)S(1)} %get-tuple-element.15.cols, bf16[8,512,256]{2,1,0:T(8,128)(2,1)S(1)} %get-tuple-element.16.rows), custom_call_target="tpu_custom_call" | custom-call | flops 4294967296 | bytes 8388608 | tf_op jit(solution)/shard_map/facet_blocks/pallas_call | solution.py:177
  20.8 0.0 copy-start.4
  20.8 0.1 collective-permute-start
  20.9 1.0 %collective-permute-start.1 = (bf16[128,512]{1,0:T(8,128)(2,1)S(1)}, bf16[128,512]{1,0:T(8,128)(2,1)S(1)}, u32[]{:S(2)}, u32[]{:S(2)}) collective-permute-start(bf16[128,512]{1,0:T(8,128)(2,1)S(1)} %get-tuple-element.19), channel_id=1, source_target_pairs={{0,2},{1,3},{2,4},{3,5},{4,6},{5,7},{6,0},{7,1},{8,10},{9,11},{10,... | collective-permute-start | bytes 393224 | tf_op jit(solution)/shard_map/ppermute | solution.py:385
  21.9 0.0 collective-permute-start.6
  21.9 0.1 pad_add_fusion.place
  21.9 1.4 %col_table.1.table = bf16[8,512,128]{2,1,0:T(8,128)(2,1)S(1)} custom-call(s32[2]{0:T(128)S(1)} %pad_add_fusion.place, bf16[128,512]{1,0:T(8,128)(2,1)S(1)} %get-tuple-element.17.after), custom_call_target="tpu_custom_call" | custom-call | flops 4194304 | bytes 1048576 | tf_op jit(solution)/shard_map/col_table/pallas_call | solution.py:387
  23.3 0.0 collective-permute-done.2.refs_2_
  23.3 6.8 %collective-permute-done.refs_0_ = bf16[128,512]{1,0:T(8,128)(2,1)S(1)} collective-permute-done((bf16[128,512]{1,0:T(8,128)(2,1)S(1)}, bf16[128,512]{1,0:T(8,128)(2,1)S(1)}, u32[]{:S(2)}, u32[]{:S(2)}) %collective-permute-start) | collective-permute-done | bytes 131104 | tf_op jit(solution)/shard_map/ppermute | solution.py:385
  30.1 0.0 collective-permute-start.3
  30.1 0.0 collective-permute-done.1.refs_1_
  30.1 0.5 collective-permute-start.4
  30.7 0.0 collective-permute-start.5
  30.7 0.0 copy-done.1
  30.7 0.0 copy-done.2
  30.7 0.0 copy-done.3
  30.7 0.0 collective-permute-done.6.refs_7_
  30.7 0.8 collective-permute-done.3.refs_4_
  31.5 0.2 collective-permute-done.4.refs_5_
  31.7 0.3 collective-permute-done.5.refs_6_
  32.0 0.7 column_sums.1.after.refs_0_
  32.7 0.7 collective-permute-start.9
  33.4 0.8 collective-permute-start.8
  34.3 1.9 %collective-permute-start.7 = (bf16[20,2048]{1,0:T(8,128)(2,1)S(1)}, bf16[20,2048]{1,0:T(8,128)(2,1)S(1)}, u32[]{:S(2)}, u32[]{:S(2)}) collective-permute-start(bf16[20,2048]{1,0:T(8,128)(2,1)S(1)} %query.1), channel_id=1, source_target_pairs={{0,2},{1,3},{2,4},{3,5},{4,6},{5,7},{6,0},{7,1},{8,10},{9,11},{10,... | collective-permute-start | bytes 245768 | tf_op jit(solution)/shard_map/ppermute | solution.py:428
  36.2 2.2 %collective-permute-done.9 = bf16[20,2048]{1,0:T(8,128)(2,1)S(1)} collective-permute-done((bf16[20,2048]{1,0:T(8,128)(2,1)S(1)}, bf16[20,2048]{1,0:T(8,128)(2,1)S(1)}, u32[]{:S(2)}, u32[]{:S(2)}) %collective-permute-start.9) | collective-permute-done | bytes 81952 | tf_op jit(solution)/shard_map/ppermute | solution.py:428
  38.4 5.4 %collective-permute-done.8 = bf16[20,2048]{1,0:T(8,128)(2,1)S(1)} collective-permute-done((bf16[20,2048]{1,0:T(8,128)(2,1)S(1)}, bf16[20,2048]{1,0:T(8,128)(2,1)S(1)}, u32[]{:S(2)}, u32[]{:S(2)}) %collective-permute-start.8) | collective-permute-done | bytes 81952 | tf_op jit(solution)/shard_map/ppermute | solution.py:428
  43.8 0.0 collective-permute-done.7
  43.8 0.1 pad_maximum_fusion.queries_own
  43.9 0.1 collective-permute-start.10
  43.9 2.5 %collective-permute-start.13 = (bf16[512,256]{1,0:T(8,128)(2,1)S(1)}, bf16[512,256]{1,0:T(8,128)(2,1)S(1)}, u32[]{:S(2)}, u32[]{:S(2)}) collective-permute-start(bf16[512,256]{1,0:T(8,128)(2,1)S(1)} %column_sums.1.after.refs_0_), channel_id=1, source_target_pairs={{0,24},{8,0},{16,8},{24,16},{1,25},{9,1},{17,9},{25,17},{2,26},{10... | collective-permute-start | bytes 786440 | tf_op jit(solution)/shard_map/ppermute | solution.py:411
  46.4 0.5 collective-permute-start.12
  46.9 0.6 collective-permute-start.11
  47.5 2.2 %row_table.1.table = bf16[8,128,1024]{2,1,0:T(8,128)(2,1)S(1)} custom-call(s32[2]{0:T(128)S(1)} %pad_add_fusion.place, bf16[512,256]{1,0:T(8,128)(2,1)S(1)} %column_sums.1.after.refs_0_), custom_call_target="tpu_custom_call" | custom-call | flops 8388608 | bytes 2097152 | tf_op jit(solution)/shard_map/row_table/pallas_call | solution.py:412
  49.8 3.4 %collective-permute-done.13.refs_3_ = bf16[512,256]{1,0:T(8,128)(2,1)S(1)} collective-permute-done((bf16[512,256]{1,0:T(8,128)(2,1)S(1)}, bf16[512,256]{1,0:T(8,128)(2,1)S(1)}, u32[]{:S(2)}, u32[]{:S(2)}) %collective-permute-start.13) | collective-permute-done | bytes 262176 | tf_op jit(solution)/shard_map/ppermute | solution.py:411
  53.2 7.3 %collective-permute-done.12.refs_2_ = bf16[512,256]{1,0:T(8,128)(2,1)S(1)} collective-permute-done((bf16[512,256]{1,0:T(8,128)(2,1)S(1)}, bf16[512,256]{1,0:T(8,128)(2,1)S(1)}, u32[]{:S(2)}, u32[]{:S(2)}) %collective-permute-start.12) | collective-permute-done | bytes 262176 | tf_op jit(solution)/shard_map/ppermute | solution.py:411
  60.4 0.0 collective-permute-done.11.refs_1_
  60.4 0.0 collective-permute-done.10.queries_other
  60.4 0.0 copy-done.4
  60.4 15.0 %degrid.1 = (f32[4,2,2048]{2,1,0:T(2,128)S(1)}, f32[4,2,2048]{2,1,0:T(2,128)S(1)}) custom-call(s32[2]{0:T(128)S(1)} %pad_add_fusion.place, s32[32]{0:T(128)S(1)} %copy-done.4, bf16[8,128,1024]{2,1,0:T(8,128)(2,1)S(1)} %row_table.1.table, bf16[4,20,2048]{2,1,0:T(8,128)(2,1)S(1)} %pad_maximum_fusion.queries_own, ...), custom_call_target="tpu_custom_call" | custom-call | flops 8589934592 | bytes 4194304 | tf_op jit(solution)/shard_map/degrid/pallas_call | solution.py:341
  75.4 0.1 collective-permute-start.14
  75.5 1.2 %collective-permute-done.14 = f32[4,2,2048]{2,1,0:T(2,128)S(1)} collective-permute-done((f32[4,2,2048]{2,1,0:T(2,128)S(1)}, f32[4,2,2048]{2,1,0:T(2,128)S(1)}, u32[]{:S(2)}, u32[]{:S(2)}) %collective-permute-start.14) | collective-permute-done | bytes 65568 | tf_op jit(solution)/shard_map/ppermute | solution.py:435
  76.8 0.1 collective-permute-start.15
  76.9 2.0 %collective-permute-start.17 = (f32[2,2048]{1,0:T(2,128)S(1)}, f32[2,2048]{1,0:T(2,128)S(1)}, u32[]{:S(2)}, u32[]{:S(2)}) collective-permute-start(f32[2,2048]{1,0:T(2,128)S(1)} %get-tuple-element.26), channel_id=1, source_target_pairs={{0,2},{1,3},{2,4},{3,5},{4,6},{5,7},{6,0},{7,1},{8,10},{9,11},{10,... | collective-permute-start | bytes 49160 | tf_op jit(solution)/shard_map/ppermute | solution.py:439
  78.9 0.0 collective-permute-start.16
  78.9 1.7 %collective-permute-done.15 = f32[2,2048]{1,0:T(2,128)S(1)} collective-permute-done((f32[2,2048]{1,0:T(2,128)S(1)}, f32[2,2048]{1,0:T(2,128)S(1)}, u32[]{:S(2)}, u32[]{:S(2)}) %collective-permute-start.15) | collective-permute-done | bytes 16416 | tf_op jit(solution)/shard_map/ppermute | solution.py:439
  80.6 1.9 %collective-permute-done.17 = f32[2,2048]{1,0:T(2,128)S(1)} collective-permute-done((f32[2,2048]{1,0:T(2,128)S(1)}, f32[2,2048]{1,0:T(2,128)S(1)}, u32[]{:S(2)}, u32[]{:S(2)}) %collective-permute-start.17) | collective-permute-done | bytes 16416 | tf_op jit(solution)/shard_map/ppermute | solution.py:439
  82.4 1.1 %collective-permute-done.16 = f32[2,2048]{1,0:T(2,128)S(1)} collective-permute-done((f32[2,2048]{1,0:T(2,128)S(1)}, f32[2,2048]{1,0:T(2,128)S(1)}, u32[]{:S(2)}, u32[]{:S(2)}) %collective-permute-start.16) | collective-permute-done | bytes 16416 | tf_op jit(solution)/shard_map/ppermute | solution.py:439
  83.5 0.6 fusion.2
  (3 shorter events, 0.1 us)
Async XLA Ops:
  0.8 4.7 %copy-start = (bf16[1024,4096]{1,0:T(8,128)(2,1)S(1)}, bf16[1024,4096]{1,0:T(8,128)(2,1)}, u32[]{:S(2)}) copy-start(bf16[1024,4096]{1,0:T(8,128)(2,1)} %sky.3) | copy-start | bytes 25165828
  10.6 20.1 %copy-start.1 = (f32[8,2048]{1,0:T(8,128)S(1)}, f32[8,2048]{1,0:T(8,128)}, u32[]{:S(2)}) copy-start(f32[8,2048]{1,0:T(8,128)} %col_kernel.1) | copy-start | bytes 196612
  10.6 20.1 %copy-start.2 = (bf16[8,2048]{1,0:T(8,128)(2,1)S(1)}, bf16[8,2048]{1,0:T(8,128)(2,1)}, u32[]{:S(2)}) copy-start(bf16[8,2048]{1,0:T(8,128)(2,1)} %row_kernel.1) | copy-start | bytes 98308
  10.6 20.0 %copy-start.3 = (s32[2,2048]{1,0:T(2,128)S(1)}, s32[2,2048]{1,0:T(2,128)}, u32[]{:S(2)}) copy-start(s32[2,2048]{1,0:T(2,128)} %vis_cells.1) | copy-start | bytes 49156
  10.6 12.7 %collective-permute-start.2 = (bf16[128,512]{1,0:T(8,128)(2,1)S(1)}, bf16[128,512]{1,0:T(8,128)(2,1)S(1)}, u32[]{:S(2)}, u32[]{:S(2)}) collective-permute-start(bf16[128,512]{1,0:T(8,128)(2,1)S(1)} %get-tuple-element.17.after), channel_id=1, source_target_pairs={{0,6},{1,7},{2,0},{3,1},{4,2},{5,3},{6,4},{7,5},{8,14},{9,15},{10,... | collective-permute-start | bytes 393224 | tf_op jit(solution)/shard_map/ppermute | solution.py:385
  20.8 39.7 %copy-start.4 = (s32[32]{0:T(128)S(1)}, s32[32]{0:T(128)}, u32[]{:S(2)}) copy-start(s32[32]{0:T(128)} %readers.1) | copy-start | bytes 388
  20.8 9.3 %collective-permute-start = (bf16[128,512]{1,0:T(8,128)(2,1)S(1)}, bf16[128,512]{1,0:T(8,128)(2,1)S(1)}, u32[]{:S(2)}, u32[]{:S(2)}) collective-permute-start(bf16[128,512]{1,0:T(8,128)(2,1)S(1)} %get-tuple-element.18), channel_id=1, source_target_pairs={{0,4},{1,5},{2,6},{3,7},{4,0},{5,1},{6,2},{7,3},{8,12},{9,13},{10,... | collective-permute-start | bytes 393224 | tf_op jit(solution)/shard_map/ppermute | solution.py:385
  20.9 9.3 %collective-permute-start.1 = (bf16[128,512]{1,0:T(8,128)(2,1)S(1)}, bf16[128,512]{1,0:T(8,128)(2,1)S(1)}, u32[]{:S(2)}, u32[]{:S(2)}) collective-permute-start(bf16[128,512]{1,0:T(8,128)(2,1)S(1)} %get-tuple-element.19), channel_id=1, source_target_pairs={{0,2},{1,3},{2,4},{3,5},{4,6},{5,7},{6,0},{7,1},{8,10},{9,11},{10,... | collective-permute-start | bytes 393224 | tf_op jit(solution)/shard_map/ppermute | solution.py:385
  21.9 8.8 %collective-permute-start.6 = (bf16[128,512]{1,0:T(8,128)(2,1)S(1)}, bf16[128,512]{1,0:T(8,128)(2,1)S(1)}, u32[]{:S(2)}, u32[]{:S(2)}) collective-permute-start(bf16[128,512]{1,0:T(8,128)(2,1)S(1)} %get-tuple-element.21.refs_3_), channel_id=1, source_target_pairs={{0,1},{1,0},{2,3},{3,2},{4,5},{5,4},{6,7},{7,6},{8,9},{9,8},{10,11... | collective-permute-start | bytes 393224 | tf_op jit(solution)/shard_map/ppermute | solution.py:406
  30.1 1.3 %collective-permute-start.3 = (bf16[128,512]{1,0:T(8,128)(2,1)S(1)}, bf16[128,512]{1,0:T(8,128)(2,1)S(1)}, u32[]{:S(2)}, u32[]{:S(2)}) collective-permute-start(bf16[128,512]{1,0:T(8,128)(2,1)S(1)} %collective-permute-done.refs_0_), channel_id=1, source_target_pairs={{0,1},{1,0},{2,3},{3,2},{4,5},{5,4},{6,7},{7,6},{8,9},{9,8},{10,11... | collective-permute-start | bytes 393224 | tf_op jit(solution)/shard_map/ppermute | solution.py:406
  30.1 1.5 %collective-permute-start.4 = (bf16[128,512]{1,0:T(8,128)(2,1)S(1)}, bf16[128,512]{1,0:T(8,128)(2,1)S(1)}, u32[]{:S(2)}, u32[]{:S(2)}) collective-permute-start(bf16[128,512]{1,0:T(8,128)(2,1)S(1)} %collective-permute-done.1.refs_1_), channel_id=1, source_target_pairs={{0,1},{1,0},{2,3},{3,2},{4,5},{5,4},{6,7},{7,6},{8,9},{9,8},{10,11... | collective-permute-start | bytes 393224 | tf_op jit(solution)/shard_map/ppermute | solution.py:406
  30.7 1.3 %collective-permute-start.5 = (bf16[128,512]{1,0:T(8,128)(2,1)S(1)}, bf16[128,512]{1,0:T(8,128)(2,1)S(1)}, u32[]{:S(2)}, u32[]{:S(2)}) collective-permute-start(bf16[128,512]{1,0:T(8,128)(2,1)S(1)} %collective-permute-done.2.refs_2_), channel_id=1, source_target_pairs={{0,1},{1,0},{2,3},{3,2},{4,5},{5,4},{6,7},{7,6},{8,9},{9,8},{10,11... | collective-permute-start | bytes 393224 | tf_op jit(solution)/shard_map/ppermute | solution.py:406
  32.7 5.7 %collective-permute-start.9 = (bf16[20,2048]{1,0:T(8,128)(2,1)S(1)}, bf16[20,2048]{1,0:T(8,128)(2,1)S(1)}, u32[]{:S(2)}, u32[]{:S(2)}) collective-permute-start(bf16[20,2048]{1,0:T(8,128)(2,1)S(1)} %query.1), channel_id=1, source_target_pairs={{0,6},{1,7},{2,0},{3,1},{4,2},{5,3},{6,4},{7,5},{8,14},{9,15},{10,... | collective-permute-start | bytes 245768 | tf_op jit(solution)/shard_map/ppermute | solution.py:428
  33.4 10.4 %collective-permute-start.8 = (bf16[20,2048]{1,0:T(8,128)(2,1)S(1)}, bf16[20,2048]{1,0:T(8,128)(2,1)S(1)}, u32[]{:S(2)}, u32[]{:S(2)}) collective-permute-start(bf16[20,2048]{1,0:T(8,128)(2,1)S(1)} %query.1), channel_id=1, source_target_pairs={{0,4},{1,5},{2,6},{3,7},{4,0},{5,1},{6,2},{7,3},{8,12},{9,13},{10,... | collective-permute-start | bytes 245768 | tf_op jit(solution)/shard_map/ppermute | solution.py:428
  34.3 9.5 %collective-permute-start.7 = (bf16[20,2048]{1,0:T(8,128)(2,1)S(1)}, bf16[20,2048]{1,0:T(8,128)(2,1)S(1)}, u32[]{:S(2)}, u32[]{:S(2)}) collective-permute-start(bf16[20,2048]{1,0:T(8,128)(2,1)S(1)} %query.1), channel_id=1, source_target_pairs={{0,2},{1,3},{2,4},{3,5},{4,6},{5,7},{6,0},{7,1},{8,10},{9,11},{10,... | collective-permute-start | bytes 245768 | tf_op jit(solution)/shard_map/ppermute | solution.py:428
  43.9 16.6 %collective-permute-start.10 = (bf16[4,20,2048]{2,1,0:T(8,128)(2,1)S(1)}, bf16[4,20,2048]{2,1,0:T(8,128)(2,1)S(1)}, u32[]{:S(2)}, u32[]{:S(2)}) collective-permute-start(bf16[4,20,2048]{2,1,0:T(8,128)(2,1)S(1)} %pad_maximum_fusion.queries_own), channel_id=1, source_target_pairs={{0,1},{1,0},{2,3},{3,2},{4,5},{5,4},{6,7},{7,6},{8,9},{9,8},{10,11... | collective-permute-start | bytes 983048 | tf_op jit(solution)/shard_map/ppermute | solution.py:430
  43.9 9.2 %collective-permute-start.13 = (bf16[512,256]{1,0:T(8,128)(2,1)S(1)}, bf16[512,256]{1,0:T(8,128)(2,1)S(1)}, u32[]{:S(2)}, u32[]{:S(2)}) collective-permute-start(bf16[512,256]{1,0:T(8,128)(2,1)S(1)} %column_sums.1.after.refs_0_), channel_id=1, source_target_pairs={{0,24},{8,0},{16,8},{24,16},{1,25},{9,1},{17,9},{25,17},{2,26},{10... | collective-permute-start | bytes 786440 | tf_op jit(solution)/shard_map/ppermute | solution.py:411
  46.4 14.0 %collective-permute-start.12 = (bf16[512,256]{1,0:T(8,128)(2,1)S(1)}, bf16[512,256]{1,0:T(8,128)(2,1)S(1)}, u32[]{:S(2)}, u32[]{:S(2)}) collective-permute-start(bf16[512,256]{1,0:T(8,128)(2,1)S(1)} %column_sums.1.after.refs_0_), channel_id=1, source_target_pairs={{0,16},{8,24},{16,0},{24,8},{1,17},{9,25},{17,1},{25,9},{2,18},{10... | collective-permute-start | bytes 786440 | tf_op jit(solution)/shard_map/ppermute | solution.py:411
  46.9 13.5 %collective-permute-start.11 = (bf16[512,256]{1,0:T(8,128)(2,1)S(1)}, bf16[512,256]{1,0:T(8,128)(2,1)S(1)}, u32[]{:S(2)}, u32[]{:S(2)}) collective-permute-start(bf16[512,256]{1,0:T(8,128)(2,1)S(1)} %column_sums.1.after.refs_0_), channel_id=1, source_target_pairs={{0,8},{8,16},{16,24},{24,0},{1,9},{9,17},{17,25},{25,1},{2,10},{10... | collective-permute-start | bytes 786440 | tf_op jit(solution)/shard_map/ppermute | solution.py:411
  75.4 1.3 %collective-permute-start.14 = (f32[4,2,2048]{2,1,0:T(2,128)S(1)}, f32[4,2,2048]{2,1,0:T(2,128)S(1)}, u32[]{:S(2)}, u32[]{:S(2)}) collective-permute-start(f32[4,2,2048]{2,1,0:T(2,128)S(1)} %get-tuple-element.24), channel_id=1, source_target_pairs={{0,1},{1,0},{2,3},{3,2},{4,5},{5,4},{6,7},{7,6},{8,9},{9,8},{10,11... | collective-permute-start | bytes 196616 | tf_op jit(solution)/shard_map/ppermute | solution.py:435
  76.8 3.8 %collective-permute-start.15 = (f32[2,2048]{1,0:T(2,128)S(1)}, f32[2,2048]{1,0:T(2,128)S(1)}, u32[]{:S(2)}, u32[]{:S(2)}) collective-permute-start(f32[2,2048]{1,0:T(2,128)S(1)} %get-tuple-element.25), channel_id=1, source_target_pairs={{0,6},{1,7},{2,0},{3,1},{4,2},{5,3},{6,4},{7,5},{8,14},{9,15},{10,... | collective-permute-start | bytes 49160 | tf_op jit(solution)/shard_map/ppermute | solution.py:439
  76.9 5.6 %collective-permute-start.17 = (f32[2,2048]{1,0:T(2,128)S(1)}, f32[2,2048]{1,0:T(2,128)S(1)}, u32[]{:S(2)}, u32[]{:S(2)}) collective-permute-start(f32[2,2048]{1,0:T(2,128)S(1)} %get-tuple-element.26), channel_id=1, source_target_pairs={{0,2},{1,3},{2,4},{3,5},{4,6},{5,7},{6,0},{7,1},{8,10},{9,11},{10,... | collective-permute-start | bytes 49160 | tf_op jit(solution)/shard_map/ppermute | solution.py:439
  78.9 4.6 %collective-permute-start.16 = (f32[2,2048]{1,0:T(2,128)S(1)}, f32[2,2048]{1,0:T(2,128)S(1)}, u32[]{:S(2)}, u32[]{:S(2)}) collective-permute-start(f32[2,2048]{1,0:T(2,128)S(1)} %get-tuple-element.27), channel_id=1, source_target_pairs={{0,4},{1,5},{2,6},{3,7},{4,0},{5,1},{6,2},{7,3},{8,12},{9,13},{10,... | collective-permute-start | bytes 49160 | tf_op jit(solution)/shard_map/ppermute | solution.py:439
where the time goes:
time: 84.3 us; the launch traced here: 84.1 us
  Pallas kernels  34 us (40%)
  waiting for transfers between devices  32.2 us (38%)
  starting transfers between devices  16 us (19%)
  other arithmetic  0.87 us (1%)
    pallas_call x1, Pallas kernels, degrid(): pl.pallas_call(functools.partial(degrid_kernel, geometry + (len(sums),)),...  15 us
    ppermute x3, waiting for transfers between devices, local(): sums.append(lax.ppermute(sums[0], 'fx', ring))  10.7 us
    pallas_call x2, Pallas kernels, facet_blocks(): pl.pallas_call(functools.partial(blocks_kernel, pair), in_specs=[VMEM] *...  10 us
    ppermute x3, waiting for transfers between devices, local(): queries.append(lax.ppermute(moved, 'fy', ring))  7.58 us
    ppermute x3, waiting for transfers between devices, local(): moved = lax.ppermute(block, 'fy', plane_shift(step, copy_step))  6.83 us
    ppermute x3, starting transfers between devices, local(): moved = lax.ppermute(block, 'fy', plane_shift(step, copy_step))  6.2 us
    pallas_call x1, Pallas kernels, strip_tables(): pl.pallas_call(functools.partial(tables_kernel, steps, geometry), in_spec...  4.73 us
    ppermute x3, waiting for transfers between devices, local(): vis = vis + lax.ppermute(both[step], 'fy', ring)  4.63 us
  transfers between devices with their start and end apart: 18, of which 12 were waited for; matrix products, arithmetic and copies ran while one was open for 0% of the time, Pallas kernels for 10%

commit v1 on v0

--- a/solution.py
+++ b/solution.py
@@ -17,7 +17,7 @@
 W = 8
 STEP = 64
 GROUP = 8
-VBLOCK = 256
+MIDDLE = (SUB - W) // 2
 HALF = SUB // 2
 F32 = jnp.float32
 BF16 = jnp.bfloat16
@@ -89,7 +89,7 @@
     lane, row = iota((STEP, K), 1), iota((STEP, K), 0)
     re, im = parts_of(0)
     for s, step in enumerate(steps):
-        chosen = (own + step) % NSUB
+        chosen = own ^ step
         pair, (out_re, out_im) = s // 2, parts_of(s % 2)
         frequency = meta[2 + NSUB + chosen] + SUB // K * lane
         coarse_col[s, :, re], coarse_col[s, :, im] = turn(
@@ -205,7 +205,7 @@
     for other in range(2):
         for step in sources:
             for copy_step in range(copies):
-                source = (own + NSUB - step) % NSUB * copies + (plane + copies - copy_step) % copies
+                source = (own ^ step) * copies + (plane % copies ^ copy_step)
                 turned = wave(steps * (2 * source + (core + other) % 2), period)
                 both = expand(real_part, imag_part, turned[0][None], turned[1][None])
                 out[at, :HALF, :] = both[0].reshape(HALF, K).astype(BF16)
@@ -225,7 +225,7 @@
     steps = gap[:period]
     for source in range(period):
         step, a = source // facets, source % facets
-        facet_row = (place[0] + rows_axis - step) % rows_axis * facets + a
+        facet_row = (place[0] ^ step) * facets + a
         turned = wave(steps * facet_row, period)
         both = expand(real_part, imag_part, turned[0][None], turned[1][None])
         out[source, :, :SUB] = both[0].reshape(K, SUB).astype(BF16)
@@ -269,35 +269,50 @@
 
 
 def query_kernel(vis_cells, row_kernel, col_kernel, after, out):
-    out[0:W, :] = row_kernel[...]
-    out[W : 2 * W, :] = col_kernel[...].astype(BF16)
-    cells = vis_cells[...]
-    halves = [cells >> 1, cells & 1]
-    cells = jnp.concatenate([half[axis : axis + 1] for axis in range(2) for half in halves])
-    out[2 * W :, :] = cells.astype(F32).astype(BF16)
-
-
-def degrid_kernel(geometry, place, readers, table, queries_own, queries_other, *refs):
-    cols_axis, copies, count = geometry
-    sums, outs, subgrid = refs[:count], refs[count : count + 2], refs[count + 2]
+    count = vis_cells.shape[1]
+    out[:, :count] = row_kernel[...]
+    out[:, count : 2 * count] = col_kernel[...].astype(BF16)
+    cells = (vis_cells[...] - MIDDLE).astype(F32)
+    quarters = [
+        cells[axis : axis + 1, at * count // 4 : (at + 1) * count // 4]
+        for axis in range(2)
+        for at in range(4)
+    ]
+    out[:, 2 * count :] = jnp.concatenate(quarters, axis=0).astype(BF16)
+
+
+def row_sums(sums, table):
+    total = None
+    facets = sums[0].shape[1] // K
+    for source, part in enumerate(sums):
+        turned = jnp.concatenate(
+            [table[at] for at in range(source * facets, (source + 1) * facets)], axis=0
+        )
+        part = jnp.dot(part[...], turned, preferred_element_type=F32)
+        total = part if total is None else total + part
+    return total
+
+
+def partial_kernel(table, *refs):
+    refs[-1][...] = row_sums(refs[:-1], table)
+
+
+def degrid_kernel(geometry, place, readers, table, partial, last, queries_own, queries_other, *refs):
+    cols_axis, copies = geometry
+    outs, subgrid = refs[:2], refs[2]
     at_x, at_y = place[0], place[1]
     plane, core = at_y // 2, at_y % 2
     own = plane // copies
-    total = None
-    facets = sums[0].shape[1] // K
-    for source in range(count):
-        turned = jnp.concatenate(
-            [table[at] for at in range(source * facets, (source + 1) * facets)], axis=0
-        )
-        part = jnp.dot(sums[source][...], turned, preferred_element_type=F32)
-        total = part if total is None else total + part
+    facets = last.shape[1] // K
+    total = partial[...] + row_sums([last], table[table.shape[0] - facets :])
     subgrid[:HALF, :] = (total[:HALF, :SUB] - total[HALF:, SUB:]).astype(BF16)
     subgrid[HALF:, :] = (total[:HALF, SUB:] + total[HALF:, :SUB]).astype(BF16)
-    planes, _, visibilities = queries_own.shape
+    planes = queries_own.shape[0]
+    count = outs[0].shape[2]
     for other, (queries, out) in enumerate(zip((queries_own, queries_other), outs)):
 
         def slot_turn(slot, carry):
-            source = (plane + planes - slot) % planes
+            source = plane ^ slot
             reader = at_x * cols_axis + 2 * source + (core + other) % 2
             active = (readers[reader] == own) & (source % copies == plane % copies)
 
@@ -307,47 +322,43 @@
 
             @pl.when(active)
             def _():
-                def block_turn(block, carry):
-                    here = pl.ds(pl.multiple_of(block * VBLOCK, VBLOCK), VBLOCK)
-                    rows = queries[slot, :, here].astype(F32)
-                    u = (rows[16:17] * 2.0 + rows[17:18]).astype(jnp.int32)
-                    w = (rows[18:19] * 2.0 + rows[19:20]).astype(jnp.int32)
-                    row_value, row_group = taps_of(u, rows[0:8], (W, VBLOCK))
-                    groups = iota((SUB // W, W, VBLOCK), 0)
-                    weights = jnp.where(groups == row_group[None], row_value[None], 0.0)
-                    weights = weights.reshape(SUB, VBLOCK).astype(BF16)
-                    spread = jnp.dot(subgrid[...], weights, preferred_element_type=F32)
-                    spread = spread.reshape(2, HALF // W, W, VBLOCK)
-                    col_value, col_group = taps_of(w, rows[8:16], (W, VBLOCK))
-                    groups = iota((HALF // W, W, VBLOCK), 0)
-                    hit = groups == (col_group - core * (HALF // W))[None]
-                    for p in range(2):
-                        picked = jnp.sum(jnp.where(hit, spread[p], 0.0), axis=0)
-                        out[slot, p : p + 1, here] = jnp.sum(
-                            picked * col_value, axis=0, keepdims=True
-                        )
-                    return carry
-
-                lax.fori_loop(0, visibilities // VBLOCK, block_turn, 0)
+                values = queries[slot].astype(F32)
+                cells = values[:, 2 * count :].astype(jnp.int32) + MIDDLE
+                u, w = [
+                    jnp.concatenate([cells[4 * axis + at : 4 * axis + at + 1] for at in range(4)], axis=1)
+                    for axis in range(2)
+                ]
+                row_value, row_group = taps_of(u, values[:, :count], (W, count))
+                groups = iota((SUB // W, W, count), 0)
+                weights = jnp.where(groups == row_group[None], row_value[None], 0.0)
+                weights = weights.reshape(SUB, count).astype(BF16)
+                spread = jnp.dot(subgrid[...], weights, preferred_element_type=F32)
+                spread = spread.reshape(2, HALF // W, W, count)
+                col_value, col_group = taps_of(w, values[:, count : 2 * count], (W, count))
+                groups = iota((HALF // W, W, count), 0)
+                hit = groups == (col_group - core * (HALF // W))[None]
+                for p in range(2):
+                    picked = jnp.sum(jnp.where(hit, spread[p], 0.0), axis=0)
+                    out[slot, p : p + 1, :] = jnp.sum(picked * col_value, axis=0, keepdims=True)
 
             return carry
 
         lax.fori_loop(0, planes, slot_turn, 0)
 
 
-def degrid(place, readers, table, queries, others, sums, geometry):
-    planes, _, visibilities = queries.shape
-    result = jax.ShapeDtypeStruct((planes, 2, visibilities), F32)
+def degrid(place, readers, table, partial, last, queries, others, geometry):
+    planes, _, width = queries.shape
+    result = jax.ShapeDtypeStruct((planes, 2, width * 4 // 9), F32)
     return pl.pallas_call(
-        functools.partial(degrid_kernel, geometry + (len(sums),)),
-        in_specs=[SMEM, SMEM] + [VMEM] * (3 + len(sums)),
+        functools.partial(degrid_kernel, geometry),
+        in_specs=[SMEM, SMEM] + [VMEM] * 5,
         out_specs=[VMEM, VMEM],
         out_shape=[result, result],
         scratch_shapes=[pltpu.VMEM((2 * HALF, SUB), BF16)],
         cost_estimate=pl.CostEstimate(flops=1 << 33, bytes_accessed=1 << 22, transcendentals=0),
-        compiler_params=pltpu.CompilerParams(vmem_limit_bytes=20 << 20),
+        compiler_params=pltpu.CompilerParams(vmem_limit_bytes=24 << 20),
         name="degrid",
-    )(place, readers, table, queries, others, *sums)
+    )(place, readers, table, partial, last, queries, others)
 
 
 def local(sky, sub_off, readers, vis_cells, row_kernel, col_kernel):
@@ -360,20 +371,22 @@
     facet_rows = facets * rows_axis
     row_spacing = sky_cells // facet_rows
     factor = 1.0 / math.sqrt(facet_rows * cols_axis)
-    assert planes == copies * NSUB and sky_cells & (sky_cells - 1) == 0
+    assert planes == copies * NSUB and not any(
+        size & (size - 1) for size in (sky_cells, rows_axis, copies)
+    )
     place = jnp.stack([lax.axis_index("fx"), lax.axis_index("fy")]).astype(jnp.int32)
     meta = jnp.concatenate([place, sub_off.reshape(-1)])
 
     def plane_shift(group_step, copy_step):
         moved = []
         for z in range(planes):
-            to = (z // copies + group_step) % NSUB * copies + (z % copies + copy_step) % copies
+            to = (z // copies ^ group_step) * copies + (z % copies ^ copy_step)
             moved += [(2 * z + c, 2 * to + c) for c in range(2)]
         return moved
 
     swap = [(i, i ^ 1) for i in range(cols_axis)]
 
-    steps = sorted(range(1, NSUB), key=lambda step: -min(step, NSUB - step)) + [0]
+    steps = [*range(2, NSUB), 1, 0]
     tables = strip_tables(meta, sky, steps, (sky_cells, row_spacing, copies))
     blocks = []
     for start in range(0, NSUB, 2):
@@ -397,18 +410,16 @@
         query_kernel,
         in_specs=[VMEM, VMEM, VMEM, ANY],
         out_specs=VMEM,
-        out_shape=jax.ShapeDtypeStruct((2 * W + 4, vis_cells.shape[1]), BF16),
+        out_shape=jax.ShapeDtypeStruct((W, vis_cells.shape[1] * 9 // 4), BF16),
         compiler_params=pltpu.CompilerParams(vmem_limit_bytes=20 << 20),
         name="query",
     )(vis_cells, row_kernel, col_kernel, pair[0])
-    last = len(blocks) - copies - 1
-    blocks[last], _ = lax.optimization_barrier((blocks[last], col_table))
+    *blocks[: 2 * copies], _ = lax.optimization_barrier((*blocks[: 2 * copies], col_table))
     blocks += [lax.ppermute(block, "fy", swap) for block in blocks]
     sums = [column_sums(col_table, blocks)]
 
     for step in range(1, rows_axis):
-        ring = [(i, (i + step) % rows_axis) for i in range(rows_axis)]
-        sums.append(lax.ppermute(sums[0], "fx", ring))
+        sums.append(lax.ppermute(sums[0], "fx", [(i, i ^ step) for i in range(rows_axis)]))
     row_table = pl.pallas_call(
         functools.partial(row_table_kernel, (sky_cells, facets, rows_axis)),
         in_specs=[SMEM, ANY],
@@ -424,18 +435,29 @@
     moved, _ = lax.optimization_barrier((query, sums[0]))
     queries = [query]
     for step in range(1, planes):
-        ring = [(i, (i + 2 * step) % cols_axis) for i in range(cols_axis)]
+        ring = [(i, i ^ 2 * step) for i in range(cols_axis)]
         queries.append(lax.ppermute(moved, "fy", ring))
     queries = jnp.stack(queries)
     others = lax.ppermute(queries, "fy", swap)
+    partial = pl.pallas_call(
+        partial_kernel,
+        in_specs=[VMEM] * rows_axis,
+        out_specs=VMEM,
+        out_shape=jax.ShapeDtypeStruct((2 * HALF, 2 * SUB), F32),
+        cost_estimate=pl.CostEstimate(
+            flops=8 * HALF * SUB * facet_rows * K, bytes_accessed=1 << 22, transcendentals=0
+        ),
+        compiler_params=pltpu.CompilerParams(vmem_limit_bytes=20 << 20),
+        name="partial_rows",
+    )(row_table, *sums[:-1])
     results, others = degrid(
-        place, readers, row_table, queries, others, sums, (cols_axis, copies)
+        place, readers, row_table, partial, sums[-1], queries, others, (cols_axis, copies)
     )
 
     both = results + lax.ppermute(others, "fy", swap)
     vis = both[0]
     for step in range(1, planes):
-        ring = [(i, (i - 2 * step) % cols_axis) for i in range(cols_axis)]
+        ring = [(i, i ^ 2 * step) for i in range(cols_axis)]
         vis = vis + lax.ppermute(both[step], "fy", ring)
     return vis
 

time: 84.3 us -> 65 us (0.77)
  waiting for transfers between devices: 32.2 us -> 14.8 us
  Pallas kernels: 34 us -> 28.1 us
  starting transfers between devices: 16 us -> 20.1 us
    ppermute x3, waiting for transfers between devices: 10.7 us -> 3.87 us  [local(): lax.ppermute(sums[0], 'fx', [(i, i ^ step) for i in range(rows_axis)])]
    pallas_call x1 -> x2, Pallas kernels: 15 us -> 9.04 us  [the longest x1 8.06 us: degrid(): pl.pallas_call(functools.partial(degrid_kernel, geometry), in_specs=[SMEM...]
    ppermute x3, waiting for transfers between devices: 7.58 us -> 2.76 us  [local(): queries.append(lax.ppermute(moved, 'fy', ring))]
    ppermute x3, waiting for transfers between devices: 6.83 us -> 3.86 us  [local(): moved = lax.ppermute(block, 'fy', plane_shift(step, copy_step))]
    ppermute x3, waiting for transfers between devices: 4.63 us -> 2.13 us  [local(): vis = vis + lax.ppermute(both[step], 'fy', ring)]
    ppermute x3, starting transfers between devices: 3.6 us -> 5.67 us  [local(): lax.ppermute(sums[0], 'fx', [(i, i ^ step) for i in range(rows_axis)])]
    ppermute x3, starting transfers between devices: 2.07 us -> 3.54 us  [local(): vis = vis + lax.ppermute(both[step], 'fy', ring)]
    ppermute x3, starting transfers between devices: 3.49 us -> 4.45 us  [local(): queries.append(lax.ppermute(moved, 'fy', ring))]
  transfers between devices with their start and end apart: 18 -> 18, of which waited for: 12 -> 9; matrix products, arithmetic and copies ran while one was open for 0% -> 0% of each run, Pallas kernels for 10% -> 15%
where the time goes in v1:
time: 65 us; the launch traced here: 64.8 us
  Pallas kernels  28.1 us (43%)
  starting transfers between devices  20.1 us (31%)
  waiting for transfers between devices  14.8 us (23%)
  other arithmetic  0.85 us (1%)
  local copies, waits for them, and re-layouts  0.79 us (1%)
    pallas_call x2, Pallas kernels, facet_blocks(): pl.pallas_call(functools.partial(blocks_kernel, pair), in_specs=[VMEM] *...  10 us
    pallas_call x1, Pallas kernels, degrid(): pl.pallas_call(functools.partial(degrid_kernel, geometry), in_specs=[SMEM...  8.06 us
    ppermute x3, starting transfers between devices, local(): moved = lax.ppermute(block, 'fy', plane_shift(step, copy_step))  5.78 us
    ppermute x3, starting transfers between devices, local(): lax.ppermute(sums[0], 'fx', [(i, i ^ step) for i in range(rows_axis)])  5.67 us
    pallas_call x1, Pallas kernels, strip_tables(): pl.pallas_call(functools.partial(tables_kernel, steps, geometry), in_spec...  4.73 us
    ppermute x3, starting transfers between devices, local(): queries.append(lax.ppermute(moved, 'fy', ring))  4.45 us
    ppermute x3, waiting for transfers between devices, local(): lax.ppermute(sums[0], 'fx', [(i, i ^ step) for i in range(rows_axis)])  3.87 us
    ppermute x3, waiting for transfers between devices, local(): moved = lax.ppermute(block, 'fy', plane_shift(step, copy_step))  3.86 us
  transfers between devices with their start and end apart: 18, of which 9 were waited for; matrix products, arithmetic and copies ran while one was open for 0% of the time, Pallas kernels for 15%

profile of v1, /device:TPU:0, one launch (start us, length us, event | category | flops | bytes accessed | tf_op | source)
XLA Modules:
  0.0 64.8 jit_solution(8128461420301364178)
XLA Ops:
  0.0 0.8 %reshape.3 = s32[8]{0:T(128)S(1)} reshape(s32[2,4]{1,0:T(2,128)} %param.7) | data formatting | bytes 64 | tf_op jit(solution)/shard_map/reshape | solution.py:378
  0.8 0.0 slice-start
  0.8 0.1 pad_add_fusion.1.meta
  0.8 0.0 slice-start.1
  0.8 4.7 %strip_tables.1 = (bf16[2,4096,512]{2,1,0:T(8,128)(2,1)S(1)}, bf16[8,512,256]{2,1,0:T(8,128)(2,1)S(1)}) custom-call(s32[10]{0:T(128)S(1)} %pad_add_fusion.1.meta), custom_call_target="tpu_custom_call" | custom-call | flops 8589934592 | bytes 16777216 | tf_op jit(solution)/shard_map/strip_tables/pallas_call | solution.py:138
  5.6 0.0 slice-done
  5.6 0.0 slice-done.1
  5.6 5.0 %facet_blocks.3 = (bf16[128,512]{1,0:T(8,128)(2,1)S(1)}, bf16[128,512]{1,0:T(8,128)(2,1)S(1)}) custom-call(bf16[1024,4096]{1,0:T(8,128)(2,1)S(1)} %bitcast.21, bf16[2,4096,512]{2,1,0:T(8,128)(2,1)S(1)} %get-tuple-element.16.cols, bf16[8,512,256]{2,1,0:T(8,128)(2,1)S(1)} %get-tuple-element.17.rows), custom_call_target="tpu_custom_call" | custom-call | flops 4294967296 | bytes 8388608 | tf_op jit(solution)/shard_map/facet_blocks/pallas_call | solution.py:177
  10.6 4.1 %collective-permute-start = (bf16[128,512]{1,0:T(8,128)(2,1)S(1)}, bf16[128,512]{1,0:T(8,128)(2,1)S(1)}, u32[]{:S(2)}, u32[]{:S(2)}) collective-permute-start(bf16[128,512]{1,0:T(8,128)(2,1)S(1)} %get-tuple-element.19), channel_id=1, source_target_pairs={{0,4},{1,5},{2,6},{3,7},{4,0},{5,1},{6,2},{7,3},{8,12},{9,13},{10,... | collective-permute-start | bytes 393224 | tf_op jit(solution)/shard_map/ppermute | solution.py:398
  14.7 0.0 copy-start
  14.7 0.0 copy-start.1
  14.7 0.0 copy-start.2
  14.8 1.3 %collective-permute-start.1 = (bf16[128,512]{1,0:T(8,128)(2,1)S(1)}, bf16[128,512]{1,0:T(8,128)(2,1)S(1)}, u32[]{:S(2)}, u32[]{:S(2)}) collective-permute-start(bf16[128,512]{1,0:T(8,128)(2,1)S(1)} %get-tuple-element.20), channel_id=1, source_target_pairs={{0,6},{1,7},{2,4},{3,5},{4,2},{5,3},{6,0},{7,1},{8,14},{9,15},{10,... | collective-permute-start | bytes 393224 | tf_op jit(solution)/shard_map/ppermute | solution.py:398
  16.1 5.0 %facet_blocks.2 = (bf16[128,512]{1,0:T(8,128)(2,1)S(1)}, bf16[128,512]{1,0:T(8,128)(2,1)S(1)}) custom-call(bf16[1024,4096]{1,0:T(8,128)(2,1)S(1)} %bitcast.21, bf16[2,4096,512]{2,1,0:T(8,128)(2,1)S(1)} %get-tuple-element.16.cols, bf16[8,512,256]{2,1,0:T(8,128)(2,1)S(1)} %get-tuple-element.17.rows), custom_call_target="tpu_custom_call" | custom-call | flops 4294967296 | bytes 8388608 | tf_op jit(solution)/shard_map/facet_blocks/pallas_call | solution.py:177
  21.1 0.3 collective-permute-start.2
  21.4 0.0 collective-permute-start.6
  21.4 0.1 pad_add_fusion.place
  21.5 1.4 %col_table.1.table = bf16[8,512,128]{2,1,0:T(8,128)(2,1)S(1)} custom-call(s32[2]{0:T(128)S(1)} %pad_add_fusion.place, bf16[128,512]{1,0:T(8,128)(2,1)S(1)} %get-tuple-element.18.after), custom_call_target="tpu_custom_call" | custom-call | flops 4194304 | bytes 1048576 | tf_op jit(solution)/shard_map/col_table/pallas_call | solution.py:400
  22.9 1.9 %collective-permute-done.refs_0_ = bf16[128,512]{1,0:T(8,128)(2,1)S(1)} collective-permute-done((bf16[128,512]{1,0:T(8,128)(2,1)S(1)}, bf16[128,512]{1,0:T(8,128)(2,1)S(1)}, u32[]{:S(2)}, u32[]{:S(2)}) %collective-permute-start) | collective-permute-done | bytes 131104 | tf_op jit(solution)/shard_map/ppermute | solution.py:398
  24.7 0.0 collective-permute-done.1.refs_1_
  24.7 0.0 collective-permute-start.3
  24.7 2.0 %collective-permute-done.2.refs_2_ = bf16[128,512]{1,0:T(8,128)(2,1)S(1)} collective-permute-done((bf16[128,512]{1,0:T(8,128)(2,1)S(1)}, bf16[128,512]{1,0:T(8,128)(2,1)S(1)}, u32[]{:S(2)}, u32[]{:S(2)}) %collective-permute-start.2) | collective-permute-done | bytes 131104 | tf_op jit(solution)/shard_map/ppermute | solution.py:398
  26.7 0.0 collective-permute-start.5
  26.7 0.5 collective-permute-start.4
  27.2 0.0 copy-done
  27.2 0.0 copy-done.1
  27.2 0.0 copy-done.2
  27.3 0.0 collective-permute-done.6.refs_7_
  27.3 0.8 %collective-permute-done.5.refs_6_ = bf16[128,512]{1,0:T(8,128)(2,1)S(1)} collective-permute-done((bf16[128,512]{1,0:T(8,128)(2,1)S(1)}, bf16[128,512]{1,0:T(8,128)(2,1)S(1)}, u32[]{:S(2)}, u32[]{:S(2)}) %collective-permute-start.5) | collective-permute-done | bytes 131104 | tf_op jit(solution)/shard_map/ppermute | solution.py:418
  28.1 0.0 collective-permute-done.3.refs_4_
  28.1 0.2 collective-permute-done.4.refs_5_
  28.3 0.7 %column_sums.1.after.refs_0_ = bf16[512,256]{1,0:T(8,128)(2,1)S(1)} custom-call(bf16[8,512,128]{2,1,0:T(8,128)(2,1)S(1)} %col_table.1.table, bf16[128,512]{1,0:T(8,128)(2,1)S(1)} %collective-permute-done.refs_0_, bf16[128,512]{1,0:T(8,128)(2,1)S(1)} %collective-permute-done.1.refs_1_, bf16[128,512]{1,0:T(8,128)(2,1)S(1)} %collective-permute-done.2.refs_2_, ...), custom_call_target="tpu_custom_call" | custom-call | flops 536870912 | bytes 2097152 | tf_op jit(solution)/shard_map/column_sums/pallas_call | solution.py:251
  29.0 3.6 %collective-permute-start.12 = (bf16[8,4608]{1,0:T(8,128)(2,1)S(1)}, bf16[8,4608]{1,0:T(8,128)(2,1)S(1)}, u32[]{:S(2)}, u32[]{:S(2)}) collective-permute-start(bf16[8,4608]{1,0:T(8,128)(2,1)S(1)} %query.1), channel_id=1, source_target_pairs={{0,6},{1,7},{2,4},{3,5},{4,2},{5,3},{6,0},{7,1},{8,14},{9,15},{10,... | collective-permute-start | bytes 221192 | tf_op jit(solution)/shard_map/ppermute | solution.py:439
  32.5 0.0 collective-permute-start.11
  32.5 0.9 %collective-permute-start.10 = (bf16[8,4608]{1,0:T(8,128)(2,1)S(1)}, bf16[8,4608]{1,0:T(8,128)(2,1)S(1)}, u32[]{:S(2)}, u32[]{:S(2)}) collective-permute-start(bf16[8,4608]{1,0:T(8,128)(2,1)S(1)} %query.1), channel_id=1, source_target_pairs={{0,2},{1,3},{2,0},{3,1},{4,6},{5,7},{6,4},{7,5},{8,10},{9,11},{10,... | collective-permute-start | bytes 221192 | tf_op jit(solution)/shard_map/ppermute | solution.py:439
  33.4 1.7 %collective-permute-start.8 = (bf16[512,256]{1,0:T(8,128)(2,1)S(1)}, bf16[512,256]{1,0:T(8,128)(2,1)S(1)}, u32[]{:S(2)}, u32[]{:S(2)}) collective-permute-start(bf16[512,256]{1,0:T(8,128)(2,1)S(1)} %column_sums.1.after.refs_0_), channel_id=1, source_target_pairs={{0,16},{8,24},{16,0},{24,8},{1,17},{9,25},{17,1},{25,9},{2,18},{10... | collective-permute-start | bytes 786440 | tf_op jit(solution)/shard_map/ppermute | solution.py:422
  35.1 1.5 %collective-permute-start.7 = (bf16[512,256]{1,0:T(8,128)(2,1)S(1)}, bf16[512,256]{1,0:T(8,128)(2,1)S(1)}, u32[]{:S(2)}, u32[]{:S(2)}) collective-permute-start(bf16[512,256]{1,0:T(8,128)(2,1)S(1)} %column_sums.1.after.refs_0_), channel_id=1, source_target_pairs={{0,8},{8,0},{16,24},{24,16},{1,9},{9,1},{17,25},{25,17},{2,10},{10... | collective-permute-start | bytes 786440 | tf_op jit(solution)/shard_map/ppermute | solution.py:422
  36.6 0.0 collective-permute-done.12
  36.6 2.8 %collective-permute-done.11 = bf16[8,4608]{1,0:T(8,128)(2,1)S(1)} collective-permute-done((bf16[8,4608]{1,0:T(8,128)(2,1)S(1)}, bf16[8,4608]{1,0:T(8,128)(2,1)S(1)}, u32[]{:S(2)}, u32[]{:S(2)}) %collective-permute-start.11) | collective-permute-done | bytes 73760 | tf_op jit(solution)/shard_map/ppermute | solution.py:439
  39.3 0.0 collective-permute-done.10
  39.4 0.1 collective-permute-start.13
  39.5 2.5 %collective-permute-start.9 = (bf16[512,256]{1,0:T(8,128)(2,1)S(1)}, bf16[512,256]{1,0:T(8,128)(2,1)S(1)}, u32[]{:S(2)}, u32[]{:S(2)}) collective-permute-start(bf16[512,256]{1,0:T(8,128)(2,1)S(1)} %column_sums.1.after.refs_0_), channel_id=1, source_target_pairs={{0,24},{8,16},{16,8},{24,0},{1,25},{9,17},{17,9},{25,1},{2,26},{10... | collective-permute-start | bytes 786440 | tf_op jit(solution)/shard_map/ppermute | solution.py:422
  42.0 2.2 %row_table.1.table = bf16[8,128,1024]{2,1,0:T(8,128)(2,1)S(1)} custom-call(s32[2]{0:T(128)S(1)} %pad_add_fusion.place, bf16[512,256]{1,0:T(8,128)(2,1)S(1)} %column_sums.1.after.refs_0_), custom_call_target="tpu_custom_call" | custom-call | flops 8388608 | bytes 2097152 | tf_op jit(solution)/shard_map/row_table/pallas_call | solution.py:423
  44.2 0.0 copy-start.3
  44.2 0.0 collective-permute-done.8.refs_2_
  44.2 0.0 collective-permute-done.7.refs_1_
  44.2 1.0 %partial_rows.1.partial = f32[512,1024]{1,0:T(8,128)S(1)} custom-call(bf16[8,128,1024]{2,1,0:T(8,128)(2,1)S(1)} %row_table.1.table, bf16[512,256]{1,0:T(8,128)(2,1)S(1)} %column_sums.1.after.refs_0_, bf16[512,256]{1,0:T(8,128)(2,1)S(1)} %collective-permute-done.7.refs_1_, bf16[512,256]{1,0:T(8,128)(2,1)S(1)} %collective-permute-done.8.refs_2_), custom_call_target="tpu_custom_call" | custom-call | flops 1073741824 | bytes 4194304 | tf_op jit(solution)/shard_map/partial_rows/pallas_call | solution.py:442
  45.2 3.9 %collective-permute-done.9.last = bf16[512,256]{1,0:T(8,128)(2,1)S(1)} collective-permute-done((bf16[512,256]{1,0:T(8,128)(2,1)S(1)}, bf16[512,256]{1,0:T(8,128)(2,1)S(1)}, u32[]{:S(2)}, u32[]{:S(2)}) %collective-permute-start.9) | collective-permute-done | bytes 262176 | tf_op jit(solution)/shard_map/ppermute | solution.py:422
  49.1 0.0 collective-permute-done.13.queries_other
  49.1 0.0 copy-done.3
  49.1 8.1 %degrid.1 = (f32[4,2,2048]{2,1,0:T(2,128)S(1)}, f32[4,2,2048]{2,1,0:T(2,128)S(1)}) custom-call(s32[2]{0:T(128)S(1)} %pad_add_fusion.place, s32[32]{0:T(128)S(1)} %copy-done.3, bf16[8,128,1024]{2,1,0:T(8,128)(2,1)S(1)} %row_table.1.table, f32[512,1024]{1,0:T(8,128)S(1)} %partial_rows.1.partial, bf16[512,256]{1,0:T(8,128)(2,1)S(1)} %collective-permute-done.9.last, ...), custom_call_target="tpu_custom_call" | custom-call | flops 8589934592 | bytes 4194304 | tf_op jit(solution)/shard_map/degrid/pallas_call | solution.py:352
  57.2 0.1 collective-permute-start.14
  57.2 1.2 %collective-permute-done.14 = f32[4,2,2048]{2,1,0:T(2,128)S(1)} collective-permute-done((f32[4,2,2048]{2,1,0:T(2,128)S(1)}, f32[4,2,2048]{2,1,0:T(2,128)S(1)}, u32[]{:S(2)}, u32[]{:S(2)}) %collective-permute-start.14) | collective-permute-done | bytes 65568 | tf_op jit(solution)/shard_map/ppermute | solution.py:457
  58.5 0.1 collective-permute-start.15
  58.6 0.1 collective-permute-start.17
  58.7 3.4 %collective-permute-start.16 = (f32[2,2048]{1,0:T(2,128)S(1)}, f32[2,2048]{1,0:T(2,128)S(1)}, u32[]{:S(2)}, u32[]{:S(2)}) collective-permute-start(f32[2,2048]{1,0:T(2,128)S(1)} %get-tuple-element.29), channel_id=1, source_target_pairs={{0,4},{1,5},{2,6},{3,7},{4,0},{5,1},{6,2},{7,3},{8,12},{9,13},{10,... | collective-permute-start | bytes 49160 | tf_op jit(solution)/shard_map/ppermute | solution.py:461
  62.1 0.2 collective-permute-done.15
  62.3 1.9 %collective-permute-done.17 = f32[2,2048]{1,0:T(2,128)S(1)} collective-permute-done((f32[2,2048]{1,0:T(2,128)S(1)}, f32[2,2048]{1,0:T(2,128)S(1)}, u32[]{:S(2)}, u32[]{:S(2)}) %collective-permute-start.17) | collective-permute-done | bytes 16416 | tf_op jit(solution)/shard_map/ppermute | solution.py:461
  64.2 0.0 collective-permute-done.16
  64.2 0.6 fusion.2
  (5 shorter events, 0.1 us)
Async XLA Ops:
  0.8 4.8 %slice-start = ((s8[8388608]{0:T(1024)(128)(4,1)}), s8[4194304]{0:T(1024)(128)(4,1)S(1)}, s32[]{:S(2)}) async-start(s8[8388608]{0:T(1024)(128)(4,1)} %bitcast.20), calls=%async_computation | async-start | bytes 8388608
  0.8 4.7 %slice-start.1 = ((s8[8388608]{0:T(1024)(128)(4,1)}), s8[4194304]{0:T(1024)(128)(4,1)S(1)}, s32[]{:S(2)}) async-start(s8[8388608]{0:T(1024)(128)(4,1)} %bitcast.20), calls=%async_computation.1 | async-start | bytes 8388608
  10.6 14.1 %collective-permute-start = (bf16[128,512]{1,0:T(8,128)(2,1)S(1)}, bf16[128,512]{1,0:T(8,128)(2,1)S(1)}, u32[]{:S(2)}, u32[]{:S(2)}) collective-permute-start(bf16[128,512]{1,0:T(8,128)(2,1)S(1)} %get-tuple-element.19), channel_id=1, source_target_pairs={{0,4},{1,5},{2,6},{3,7},{4,0},{5,1},{6,2},{7,3},{8,12},{9,13},{10,... | collective-permute-start | bytes 393224 | tf_op jit(solution)/shard_map/ppermute | solution.py:398
  14.7 12.5 %copy-start = (f32[8,2048]{1,0:T(8,128)S(1)}, f32[8,2048]{1,0:T(8,128)}, u32[]{:S(2)}) copy-start(f32[8,2048]{1,0:T(8,128)} %col_kernel.1) | copy-start | bytes 196612
  14.7 12.5 %copy-start.1 = (bf16[8,2048]{1,0:T(8,128)(2,1)S(1)}, bf16[8,2048]{1,0:T(8,128)(2,1)}, u32[]{:S(2)}) copy-start(bf16[8,2048]{1,0:T(8,128)(2,1)} %row_kernel.1) | copy-start | bytes 98308
  14.7 12.5 %copy-start.2 = (s32[2,2048]{1,0:T(2,128)S(1)}, s32[2,2048]{1,0:T(2,128)}, u32[]{:S(2)}) copy-start(s32[2,2048]{1,0:T(2,128)} %vis_cells.1) | copy-start | bytes 49156
  14.8 10.0 %collective-permute-start.1 = (bf16[128,512]{1,0:T(8,128)(2,1)S(1)}, bf16[128,512]{1,0:T(8,128)(2,1)S(1)}, u32[]{:S(2)}, u32[]{:S(2)}) collective-permute-start(bf16[128,512]{1,0:T(8,128)(2,1)S(1)} %get-tuple-element.20), channel_id=1, source_target_pairs={{0,6},{1,7},{2,4},{3,5},{4,2},{5,3},{6,0},{7,1},{8,14},{9,15},{10,... | collective-permute-start | bytes 393224 | tf_op jit(solution)/shard_map/ppermute | solution.py:398
  21.1 5.6 %collective-permute-start.2 = (bf16[128,512]{1,0:T(8,128)(2,1)S(1)}, bf16[128,512]{1,0:T(8,128)(2,1)S(1)}, u32[]{:S(2)}, u32[]{:S(2)}) collective-permute-start(bf16[128,512]{1,0:T(8,128)(2,1)S(1)} %get-tuple-element.18.after), channel_id=1, source_target_pairs={{0,2},{1,3},{2,0},{3,1},{4,6},{5,7},{6,4},{7,5},{8,10},{9,11},{10,... | collective-permute-start | bytes 393224 | tf_op jit(solution)/shard_map/ppermute | solution.py:398
  21.4 5.8 %collective-permute-start.6 = (bf16[128,512]{1,0:T(8,128)(2,1)S(1)}, bf16[128,512]{1,0:T(8,128)(2,1)S(1)}, u32[]{:S(2)}, u32[]{:S(2)}) collective-permute-start(bf16[128,512]{1,0:T(8,128)(2,1)S(1)} %get-tuple-element.23.refs_3_), channel_id=1, source_target_pairs={{0,1},{1,0},{2,3},{3,2},{4,5},{5,4},{6,7},{7,6},{8,9},{9,8},{10,11... | collective-permute-start | bytes 393224 | tf_op jit(solution)/shard_map/ppermute | solution.py:418
  24.7 3.4 %collective-permute-start.3 = (bf16[128,512]{1,0:T(8,128)(2,1)S(1)}, bf16[128,512]{1,0:T(8,128)(2,1)S(1)}, u32[]{:S(2)}, u32[]{:S(2)}) collective-permute-start(bf16[128,512]{1,0:T(8,128)(2,1)S(1)} %collective-permute-done.refs_0_), channel_id=1, source_target_pairs={{0,1},{1,0},{2,3},{3,2},{4,5},{5,4},{6,7},{7,6},{8,9},{9,8},{10,11... | collective-permute-start | bytes 393224 | tf_op jit(solution)/shard_map/ppermute | solution.py:418
  26.7 1.3 %collective-permute-start.5 = (bf16[128,512]{1,0:T(8,128)(2,1)S(1)}, bf16[128,512]{1,0:T(8,128)(2,1)S(1)}, u32[]{:S(2)}, u32[]{:S(2)}) collective-permute-start(bf16[128,512]{1,0:T(8,128)(2,1)S(1)} %collective-permute-done.2.refs_2_), channel_id=1, source_target_pairs={{0,1},{1,0},{2,3},{3,2},{4,5},{5,4},{6,7},{7,6},{8,9},{9,8},{10,11... | collective-permute-start | bytes 393224 | tf_op jit(solution)/shard_map/ppermute | solution.py:418
  26.7 1.5 %collective-permute-start.4 = (bf16[128,512]{1,0:T(8,128)(2,1)S(1)}, bf16[128,512]{1,0:T(8,128)(2,1)S(1)}, u32[]{:S(2)}, u32[]{:S(2)}) collective-permute-start(bf16[128,512]{1,0:T(8,128)(2,1)S(1)} %collective-permute-done.1.refs_1_), channel_id=1, source_target_pairs={{0,1},{1,0},{2,3},{3,2},{4,5},{5,4},{6,7},{7,6},{8,9},{9,8},{10,11... | collective-permute-start | bytes 393224 | tf_op jit(solution)/shard_map/ppermute | solution.py:418
  29.0 7.6 %collective-permute-start.12 = (bf16[8,4608]{1,0:T(8,128)(2,1)S(1)}, bf16[8,4608]{1,0:T(8,128)(2,1)S(1)}, u32[]{:S(2)}, u32[]{:S(2)}) collective-permute-start(bf16[8,4608]{1,0:T(8,128)(2,1)S(1)} %query.1), channel_id=1, source_target_pairs={{0,6},{1,7},{2,4},{3,5},{4,2},{5,3},{6,0},{7,1},{8,14},{9,15},{10,... | collective-permute-start | bytes 221192 | tf_op jit(solution)/shard_map/ppermute | solution.py:439
  32.5 6.8 %collective-permute-start.11 = (bf16[8,4608]{1,0:T(8,128)(2,1)S(1)}, bf16[8,4608]{1,0:T(8,128)(2,1)S(1)}, u32[]{:S(2)}, u32[]{:S(2)}) collective-permute-start(bf16[8,4608]{1,0:T(8,128)(2,1)S(1)} %query.1), channel_id=1, source_target_pairs={{0,4},{1,5},{2,6},{3,7},{4,0},{5,1},{6,2},{7,3},{8,12},{9,13},{10,... | collective-permute-start | bytes 221192 | tf_op jit(solution)/shard_map/ppermute | solution.py:439
  32.5 6.8 %collective-permute-start.10 = (bf16[8,4608]{1,0:T(8,128)(2,1)S(1)}, bf16[8,4608]{1,0:T(8,128)(2,1)S(1)}, u32[]{:S(2)}, u32[]{:S(2)}) collective-permute-start(bf16[8,4608]{1,0:T(8,128)(2,1)S(1)} %query.1), channel_id=1, source_target_pairs={{0,2},{1,3},{2,0},{3,1},{4,6},{5,7},{6,4},{7,5},{8,10},{9,11},{10,... | collective-permute-start | bytes 221192 | tf_op jit(solution)/shard_map/ppermute | solution.py:439
  33.4 10.8 %collective-permute-start.8 = (bf16[512,256]{1,0:T(8,128)(2,1)S(1)}, bf16[512,256]{1,0:T(8,128)(2,1)S(1)}, u32[]{:S(2)}, u32[]{:S(2)}) collective-permute-start(bf16[512,256]{1,0:T(8,128)(2,1)S(1)} %column_sums.1.after.refs_0_), channel_id=1, source_target_pairs={{0,16},{8,24},{16,0},{24,8},{1,17},{9,25},{17,1},{25,9},{2,18},{10... | collective-permute-start | bytes 786440 | tf_op jit(solution)/shard_map/ppermute | solution.py:422
  35.1 9.1 %collective-permute-start.7 = (bf16[512,256]{1,0:T(8,128)(2,1)S(1)}, bf16[512,256]{1,0:T(8,128)(2,1)S(1)}, u32[]{:S(2)}, u32[]{:S(2)}) collective-permute-start(bf16[512,256]{1,0:T(8,128)(2,1)S(1)} %column_sums.1.after.refs_0_), channel_id=1, source_target_pairs={{0,8},{8,0},{16,24},{24,16},{1,9},{9,1},{17,25},{25,17},{2,10},{10... | collective-permute-start | bytes 786440 | tf_op jit(solution)/shard_map/ppermute | solution.py:422
  39.4 9.7 %collective-permute-start.13 = (bf16[4,8,4608]{2,1,0:T(8,128)(2,1)S(1)}, bf16[4,8,4608]{2,1,0:T(8,128)(2,1)S(1)}, u32[]{:S(2)}, u32[]{:S(2)}) collective-permute-start(bf16[4,8,4608]{2,1,0:T(8,128)(2,1)S(1)} %pad_maximum_fusion.queries_own), channel_id=1, source_target_pairs={{0,1},{1,0},{2,3},{3,2},{4,5},{5,4},{6,7},{7,6},{8,9},{9,8},{10,11... | collective-permute-start | bytes 884744 | tf_op jit(solution)/shard_map/ppermute | solution.py:441
  39.5 9.6 %collective-permute-start.9 = (bf16[512,256]{1,0:T(8,128)(2,1)S(1)}, bf16[512,256]{1,0:T(8,128)(2,1)S(1)}, u32[]{:S(2)}, u32[]{:S(2)}) collective-permute-start(bf16[512,256]{1,0:T(8,128)(2,1)S(1)} %column_sums.1.after.refs_0_), channel_id=1, source_target_pairs={{0,24},{8,16},{16,8},{24,0},{1,25},{9,17},{17,9},{25,1},{2,26},{10... | collective-permute-start | bytes 786440 | tf_op jit(solution)/shard_map/ppermute | solution.py:422
  44.2 4.9 %copy-start.3 = (s32[32]{0:T(128)S(1)}, s32[32]{0:T(128)}, u32[]{:S(2)}) copy-start(s32[32]{0:T(128)} %readers.1) | copy-start | bytes 388
  57.2 1.3 %collective-permute-start.14 = (f32[4,2,2048]{2,1,0:T(2,128)S(1)}, f32[4,2,2048]{2,1,0:T(2,128)S(1)}, u32[]{:S(2)}, u32[]{:S(2)}) collective-permute-start(f32[4,2,2048]{2,1,0:T(2,128)S(1)} %get-tuple-element.26), channel_id=1, source_target_pairs={{0,1},{1,0},{2,3},{3,2},{4,5},{5,4},{6,7},{7,6},{8,9},{9,8},{10,11... | collective-permute-start | bytes 196616 | tf_op jit(solution)/shard_map/ppermute | solution.py:457
  58.5 3.8 %collective-permute-start.15 = (f32[2,2048]{1,0:T(2,128)S(1)}, f32[2,2048]{1,0:T(2,128)S(1)}, u32[]{:S(2)}, u32[]{:S(2)}) collective-permute-start(f32[2,2048]{1,0:T(2,128)S(1)} %get-tuple-element.27), channel_id=1, source_target_pairs={{0,2},{1,3},{2,0},{3,1},{4,6},{5,7},{6,4},{7,5},{8,10},{9,11},{10,... | collective-permute-start | bytes 49160 | tf_op jit(solution)/shard_map/ppermute | solution.py:461
  58.6 5.6 %collective-permute-start.17 = (f32[2,2048]{1,0:T(2,128)S(1)}, f32[2,2048]{1,0:T(2,128)S(1)}, u32[]{:S(2)}, u32[]{:S(2)}) collective-permute-start(f32[2,2048]{1,0:T(2,128)S(1)} %get-tuple-element.28), channel_id=1, source_target_pairs={{0,6},{1,7},{2,4},{3,5},{4,2},{5,3},{6,0},{7,1},{8,14},{9,15},{10,... | collective-permute-start | bytes 49160 | tf_op jit(solution)/shard_map/ppermute | solution.py:461
  58.7 5.5 %collective-permute-start.16 = (f32[2,2048]{1,0:T(2,128)S(1)}, f32[2,2048]{1,0:T(2,128)S(1)}, u32[]{:S(2)}, u32[]{:S(2)}) collective-permute-start(f32[2,2048]{1,0:T(2,128)S(1)} %get-tuple-element.29), channel_id=1, source_target_pairs={{0,4},{1,5},{2,6},{3,7},{4,0},{5,1},{6,2},{7,3},{8,12},{9,13},{10,... | collective-permute-start | bytes 49160 | tf_op jit(solution)/shard_map/ppermute | solution.py:461

commit v2 on v1

--- a/solution.py
+++ b/solution.py
@@ -17,6 +17,7 @@
 W = 8
 STEP = 64
 GROUP = 8
+TILE = 16
 MIDDLE = (SUB - W) // 2
 HALF = SUB // 2
 F32 = jnp.float32
@@ -82,7 +83,7 @@
 
 def tables_kernel(steps, geometry, meta, out_cols, out_rows, coarse_col, fine_col):
     sky_cells, row_spacing, copies = geometry
-    count, columns = len(steps), out_cols.shape[1]
+    count, columns = len(steps), out_cols.shape[0]
     facets = out_rows.shape[0] // count
     at_x, at_y = meta[0], meta[1]
     own = at_y // 2 // copies
@@ -90,7 +91,7 @@
     re, im = parts_of(0)
     for s, step in enumerate(steps):
         chosen = own ^ step
-        pair, (out_re, out_im) = s // 2, parts_of(s % 2)
+        out_re, out_im = parts_of(s)
         frequency = meta[2 + NSUB + chosen] + SUB // K * lane
         coarse_col[s, :, re], coarse_col[s, :, im] = turn(
             frequency, at_y * FACET + STEP * row, sky_cells, 1.0 / math.sqrt(FACET)
@@ -99,16 +100,18 @@
 
         def table_turn(group, carry):
             coarse = coarse_col[s, pl.ds(pl.multiple_of(group * GROUP, GROUP), GROUP), :]
-            for piece in range(GROUP):
-                here = pl.ds(pl.multiple_of((group * GROUP + piece) * STEP, STEP), STEP)
-                real_part, imag_part = expand(
-                    coarse[piece : piece + 1, re],
-                    coarse[piece : piece + 1, im],
-                    fine_col[:, re],
-                    fine_col[:, im],
-                )
-                out_cols[pair, here, out_re] = real_part.astype(BF16)
-                out_cols[pair, here, out_im] = imag_part.astype(BF16)
+            for tile in range(0, STEP, TILE):
+                fine_real, fine_imag = fine_col[tile : tile + TILE, re], fine_col[tile : tile + TILE, im]
+                for piece in range(GROUP):
+                    here = pl.ds(pl.multiple_of((group * GROUP + piece) * STEP + tile, TILE), TILE)
+                    real_part, imag_part = expand(
+                        coarse[piece : piece + 1, re],
+                        coarse[piece : piece + 1, im],
+                        fine_real,
+                        fine_imag,
+                    )
+                    out_cols[here, out_re] = real_part.astype(BF16)
+                    out_cols[here, out_im] = imag_part.astype(BF16)
             return carry
 
         lax.fori_loop(0, columns // (STEP * GROUP), table_turn, 0)
@@ -140,7 +143,7 @@
         in_specs=[SMEM],
         out_specs=[VMEM] * 2,
         out_shape=[
-            jax.ShapeDtypeStruct((count // 2, columns, 4 * K), BF16),
+            jax.ShapeDtypeStruct((columns, 2 * count * K), BF16),
             jax.ShapeDtypeStruct((count * facets, FR, 2 * K), BF16),
         ],
         scratch_shapes=[
@@ -153,34 +156,32 @@
     )(meta)
 
 
-def blocks_kernel(pair, sky, cols, rows, *outs):
+def blocks_kernel(at, sky, cols, rows, out):
     facets = sky.shape[0] // FR
+    strips = jnp.dot(
+        sky[...], cols[:, 2 * at * K : 2 * (at + 1) * K], preferred_element_type=F32
+    ).astype(BF16)
     for a in range(facets):
-        strips = jnp.dot(
-            sky[a * FR : (a + 1) * FR, :], cols[pair], preferred_element_type=F32
-        ).astype(BF16)
-        for s in range(2):
-            product = lax.dot_general(
-                strips[:, 2 * s * K : (2 * s + 2) * K],
-                rows[(2 * pair + s) * facets + a],
-                (((0,), (0,)), ((), ())),
-                preferred_element_type=F32,
-            )
-            re, im = parts_of(a)
-            outs[s][:, re] = (product[:K, :K] - product[K:, K:]).astype(BF16)
-            outs[s][:, im] = (product[:K, K:] + product[K:, :K]).astype(BF16)
-
-
-def facet_blocks(sky, tables, pair):
+        product = lax.dot_general(
+            strips[a * FR : (a + 1) * FR, :],
+            rows[at * facets + a],
+            (((0,), (0,)), ((), ())),
+            preferred_element_type=F32,
+        )
+        re, im = parts_of(a)
+        out[:, re] = (product[:K, :K] - product[K:, K:]).astype(BF16)
+        out[:, im] = (product[:K, K:] + product[K:, :K]).astype(BF16)
+
+
+def facet_blocks(sky, tables, at):
     rows, columns = sky.shape
-    facets = rows // FR
     return pl.pallas_call(
-        functools.partial(blocks_kernel, pair),
+        functools.partial(blocks_kernel, at),
         in_specs=[VMEM] * 3,
-        out_specs=[VMEM] * 2,
-        out_shape=[jax.ShapeDtypeStruct((K, 2 * facets * K), BF16)] * 2,
+        out_specs=VMEM,
+        out_shape=jax.ShapeDtypeStruct((K, 2 * rows // FR * K), BF16),
         cost_estimate=pl.CostEstimate(
-            flops=8 * rows * columns * K, bytes_accessed=2 * rows * columns, transcendentals=0
+            flops=4 * rows * columns * K, bytes_accessed=2 * rows * columns, transcendentals=0
         ),
         compiler_params=pltpu.CompilerParams(vmem_limit_bytes=28 << 20),
         name="facet_blocks",
@@ -387,16 +388,17 @@
     swap = [(i, i ^ 1) for i in range(cols_axis)]
 
     steps = [*range(2, NSUB), 1, 0]
-    tables = strip_tables(meta, sky, steps, (sky_cells, row_spacing, copies))
     blocks = []
     for start in range(0, NSUB, 2):
-        pair = facet_blocks(sky, tables, start // 2)
-        for step, block in zip(steps[start : start + 2], pair):
+        tables = strip_tables(meta, sky, steps[start : start + 2], (sky_cells, row_spacing, copies))
+        for at, step in enumerate(steps[start : start + 2]):
+            block = facet_blocks(sky, tables, at)
             for copy_step in range(copies):
                 moved = block
                 if step or copy_step:
                     moved = lax.ppermute(block, "fy", plane_shift(step, copy_step))
                 blocks.append(moved)
+
     col_table = pl.pallas_call(
         functools.partial(col_table_kernel, (sky_cells, copies, steps), factor),
         in_specs=[SMEM, ANY],
@@ -405,7 +407,7 @@
         cost_estimate=pl.CostEstimate(flops=1 << 22, bytes_accessed=1 << 20, transcendentals=1 << 20),
         compiler_params=pltpu.CompilerParams(vmem_limit_bytes=20 << 20),
         name="col_table",
-    )(place, pair[0])
+    )(place, block)
     query = pl.pallas_call(
         query_kernel,
         in_specs=[VMEM, VMEM, VMEM, ANY],
@@ -413,7 +415,7 @@
         out_shape=jax.ShapeDtypeStruct((W, vis_cells.shape[1] * 9 // 4), BF16),
         compiler_params=pltpu.CompilerParams(vmem_limit_bytes=20 << 20),
         name="query",
-    )(vis_cells, row_kernel, col_kernel, pair[0])
+    )(vis_cells, row_kernel, col_kernel, block)
     *blocks[: 2 * copies], _ = lax.optimization_barrier((*blocks[: 2 * copies], col_table))
     blocks += [lax.ppermute(block, "fy", swap) for block in blocks]
     sums = [column_sums(col_table, blocks)]

time: 65 us -> 63.8 us (0.982)
  waiting for transfers between devices: 14.8 us -> 11.3 us
  local copies, waits for them, and re-layouts: 0.79 us -> 1.85 us
    ppermute x3, waiting for transfers between devices: 3.86 us -> 0.01 us  [local(): moved = lax.ppermute(block, 'fy', plane_shift(step, copy_step))]
    unnamed x12, local copies, waits for them, and re-layouts: 0.02 us -> 1.09 us
    pallas_call x2 -> x4, Pallas kernels: 10 us -> 10.8 us  [facet_blocks(): pl.pallas_call(functools.partial(blocks_kernel, at), in_specs=[VMEM] * 3,...]
    pallas_call x1 -> x2, Pallas kernels: 4.73 us -> 4.84 us  [strip_tables(): pl.pallas_call(functools.partial(tables_kernel, steps, geometry), in_spec...]
  transfers between devices with their start and end apart: 18 -> 18, of which waited for: 9 -> 7; matrix products, arithmetic and copies ran while one was open for 0% -> 0% of each run, Pallas kernels for 15% -> 24%
where the time goes in v2:
time: 63.8 us; the launch traced here: 63.6 us
  Pallas kernels  28.7 us (45%)
  starting transfers between devices  20.6 us (32%)
  waiting for transfers between devices  11.3 us (18%)
  local copies, waits for them, and re-layouts  1.85 us (3%)
  other arithmetic  0.85 us (1%)
    pallas_call x4, Pallas kernels, facet_blocks(): pl.pallas_call(functools.partial(blocks_kernel, at), in_specs=[VMEM] * 3,...  10.8 us
    pallas_call x1, Pallas kernels, degrid(): pl.pallas_call(functools.partial(degrid_kernel, geometry), in_specs=[SMEM...  7.87 us
    ppermute x3, starting transfers between devices, local(): moved = lax.ppermute(block, 'fy', plane_shift(step, copy_step))  5.85 us
    ppermute x3, starting transfers between devices, local(): lax.ppermute(sums[0], 'fx', [(i, i ^ step) for i in range(rows_axis)])  5.52 us
    pallas_call x2, Pallas kernels, strip_tables(): pl.pallas_call(functools.partial(tables_kernel, steps, geometry), in_spec...  4.84 us
    ppermute x3, starting transfers between devices, local(): queries.append(lax.ppermute(moved, 'fy', ring))  4.45 us
    ppermute x3, waiting for transfers between devices, local(): lax.ppermute(sums[0], 'fx', [(i, i ^ step) for i in range(rows_axis)])  3.88 us
    ppermute x3, starting transfers between devices, local(): vis = vis + lax.ppermute(both[step], 'fy', ring)  3.54 us
  transfers between devices with their start and end apart: 18, of which 7 were waited for; matrix products, arithmetic and copies ran while one was open for 0% of the time, Pallas kernels for 24%

profile of v2, /device:TPU:0, one launch (start us, length us, event | category | flops | bytes accessed | tf_op | source)
XLA Modules:
  0.0 63.6 jit_solution(262215292988524787)
XLA Ops:
  0.0 0.8 %reshape.3 = s32[8]{0:T(128)S(1)} reshape(s32[2,4]{1,0:T(2,128)} %param.7) | data formatting | bytes 64 | tf_op jit(solution)/shard_map/reshape | solution.py:379
  0.8 0.0 slice-start
  0.8 0.1 pad_add_fusion.1.meta
  0.8 0.0 slice-start.1
  0.8 2.3 %strip_tables.3 = (bf16[4096,512]{1,0:T(8,128)(2,1)S(1)}, bf16[4,512,256]{2,1,0:T(8,128)(2,1)S(1)}) custom-call(s32[10]{0:T(128)S(1)} %pad_add_fusion.1.meta), custom_call_target="tpu_custom_call" | custom-call | flops 8589934592 | bytes 16777216 | tf_op jit(solution)/shard_map/strip_tables/pallas_call | solution.py:141
  3.2 0.0 slice-done
  3.2 1.1 %slice-done.1 = s8[4194304]{0:T(1024)(128)(4,1)S(1)} async-done(((s8[8388608]{0:T(1024)(128)(4,1)}), s8[4194304]{0:T(1024)(128)(4,1)S(1)}, s32[]{:S(2)}) %slice-start.1) | async-done | bytes 4194328
  4.2 2.7 %facet_blocks.5 = bf16[128,512]{1,0:T(8,128)(2,1)S(1)} custom-call(bf16[1024,4096]{1,0:T(8,128)(2,1)S(1)} %bitcast.21, bf16[4096,512]{1,0:T(8,128)(2,1)S(1)} %get-tuple-element.16.cols, bf16[4,512,256]{2,1,0:T(8,128)(2,1)S(1)} %get-tuple-element.17.rows), custom_call_target="tpu_custom_call" | custom-call | flops 2147483648 | bytes 8388608 | tf_op jit(solution)/shard_map/facet_blocks/pallas_call | solution.py:178
  6.9 4.1 %collective-permute-start = (bf16[128,512]{1,0:T(8,128)(2,1)S(1)}, bf16[128,512]{1,0:T(8,128)(2,1)S(1)}, u32[]{:S(2)}, u32[]{:S(2)}) collective-permute-start(bf16[128,512]{1,0:T(8,128)(2,1)S(1)} %facet_blocks.5), channel_id=1, source_target_pairs={{0,4},{1,5},{2,6},{3,7},{4,0},{5,1},{6,2},{7,3},{8,12},{9,13},{10,... | collective-permute-start | bytes 393224 | tf_op jit(solution)/shard_map/ppermute | solution.py:399
  11.1 2.7 %facet_blocks.6 = bf16[128,512]{1,0:T(8,128)(2,1)S(1)} custom-call(bf16[1024,4096]{1,0:T(8,128)(2,1)S(1)} %bitcast.21, bf16[4096,512]{1,0:T(8,128)(2,1)S(1)} %get-tuple-element.16.cols, bf16[4,512,256]{2,1,0:T(8,128)(2,1)S(1)} %get-tuple-element.17.rows), custom_call_target="tpu_custom_call" | custom-call | flops 2147483648 | bytes 8388608 | tf_op jit(solution)/shard_map/facet_blocks/pallas_call | solution.py:178
  13.8 1.4 %collective-permute-start.1 = (bf16[128,512]{1,0:T(8,128)(2,1)S(1)}, bf16[128,512]{1,0:T(8,128)(2,1)S(1)}, u32[]{:S(2)}, u32[]{:S(2)}) collective-permute-start(bf16[128,512]{1,0:T(8,128)(2,1)S(1)} %facet_blocks.6), channel_id=1, source_target_pairs={{0,6},{1,7},{2,4},{3,5},{4,2},{5,3},{6,0},{7,1},{8,14},{9,15},{10,... | collective-permute-start | bytes 393224 | tf_op jit(solution)/shard_map/ppermute | solution.py:399
  15.2 2.5 %strip_tables.2 = (bf16[4096,512]{1,0:T(8,128)(2,1)S(1)}, bf16[4,512,256]{2,1,0:T(8,128)(2,1)S(1)}) custom-call(s32[10]{0:T(128)S(1)} %pad_add_fusion.1.meta), custom_call_target="tpu_custom_call" | custom-call | flops 8589934592 | bytes 16777216 | tf_op jit(solution)/shard_map/strip_tables/pallas_call | solution.py:141
  17.7 2.7 %facet_blocks.7 = bf16[128,512]{1,0:T(8,128)(2,1)S(1)} custom-call(bf16[1024,4096]{1,0:T(8,128)(2,1)S(1)} %bitcast.21, bf16[4096,512]{1,0:T(8,128)(2,1)S(1)} %get-tuple-element.14.cols, bf16[4,512,256]{2,1,0:T(8,128)(2,1)S(1)} %get-tuple-element.15.rows), custom_call_target="tpu_custom_call" | custom-call | flops 2147483648 | bytes 8388608 | tf_op jit(solution)/shard_map/facet_blocks/pallas_call | solution.py:178
  20.4 0.0 copy-start
  20.4 0.0 copy-start.1
  20.4 0.0 copy-start.2
  20.4 0.3 collective-permute-start.2
  20.7 2.7 %facet_blocks.4.after.refs_3_ = bf16[128,512]{1,0:T(8,128)(2,1)S(1)} custom-call(bf16[1024,4096]{1,0:T(8,128)(2,1)S(1)} %bitcast.21, bf16[4096,512]{1,0:T(8,128)(2,1)S(1)} %get-tuple-element.14.cols, bf16[4,512,256]{2,1,0:T(8,128)(2,1)S(1)} %get-tuple-element.15.rows), custom_call_target="tpu_custom_call" | custom-call | flops 2147483648 | bytes 8388608 | tf_op jit(solution)/shard_map/facet_blocks/pallas_call | solution.py:178
  23.4 0.1 collective-permute-start.6
  23.5 0.1 pad_add_fusion.place
  23.6 1.4 %col_table.1.table = bf16[8,512,128]{2,1,0:T(8,128)(2,1)S(1)} custom-call(s32[2]{0:T(128)S(1)} %pad_add_fusion.place, bf16[128,512]{1,0:T(8,128)(2,1)S(1)} %facet_blocks.4.after.refs_3_), custom_call_target="tpu_custom_call" | custom-call | flops 4194304 | bytes 1048576 | tf_op jit(solution)/shard_map/col_table/pallas_call | solution.py:402
  25.0 0.0 collective-permute-done.refs_0_
  25.0 0.0 collective-permute-done.1.refs_1_
  25.0 0.6 collective-permute-start.3
  25.5 0.0 collective-permute-done.2.refs_2_
  25.5 0.1 collective-permute-start.5
  25.6 0.4 collective-permute-start.4
  26.0 0.0 copy-done
  26.1 0.0 copy-done.1
  26.1 0.0 copy-done.2
  26.1 0.0 collective-permute-done.6.refs_7_
  26.1 0.8 %collective-permute-done.5.refs_6_ = bf16[128,512]{1,0:T(8,128)(2,1)S(1)} collective-permute-done((bf16[128,512]{1,0:T(8,128)(2,1)S(1)}, bf16[128,512]{1,0:T(8,128)(2,1)S(1)}, u32[]{:S(2)}, u32[]{:S(2)}) %collective-permute-start.5) | collective-permute-done | bytes 131104 | tf_op jit(solution)/shard_map/ppermute | solution.py:420
  26.9 0.0 collective-permute-done.3.refs_4_
  26.9 0.2 collective-permute-done.4.refs_5_
  27.1 0.7 %column_sums.1.after.refs_0_ = bf16[512,256]{1,0:T(8,128)(2,1)S(1)} custom-call(bf16[8,512,128]{2,1,0:T(8,128)(2,1)S(1)} %col_table.1.table, bf16[128,512]{1,0:T(8,128)(2,1)S(1)} %collective-permute-done.refs_0_, bf16[128,512]{1,0:T(8,128)(2,1)S(1)} %collective-permute-done.1.refs_1_, bf16[128,512]{1,0:T(8,128)(2,1)S(1)} %collective-permute-done.2.refs_2_, ...), custom_call_target="tpu_custom_call" | custom-call | flops 536870912 | bytes 2097152 | tf_op jit(solution)/shard_map/column_sums/pallas_call | solution.py:252
  27.8 3.0 %collective-permute-start.12 = (bf16[8,4608]{1,0:T(8,128)(2,1)S(1)}, bf16[8,4608]{1,0:T(8,128)(2,1)S(1)}, u32[]{:S(2)}, u32[]{:S(2)}) collective-permute-start(bf16[8,4608]{1,0:T(8,128)(2,1)S(1)} %query.1), channel_id=1, source_target_pairs={{0,6},{1,7},{2,4},{3,5},{4,2},{5,3},{6,0},{7,1},{8,14},{9,15},{10,... | collective-permute-start | bytes 221192 | tf_op jit(solution)/shard_map/ppermute | solution.py:441
  30.8 0.3 collective-permute-start.11
  31.1 1.1 %collective-permute-start.10 = (bf16[8,4608]{1,0:T(8,128)(2,1)S(1)}, bf16[8,4608]{1,0:T(8,128)(2,1)S(1)}, u32[]{:S(2)}, u32[]{:S(2)}) collective-permute-start(bf16[8,4608]{1,0:T(8,128)(2,1)S(1)} %query.1), channel_id=1, source_target_pairs={{0,2},{1,3},{2,0},{3,1},{4,6},{5,7},{6,4},{7,5},{8,10},{9,11},{10,... | collective-permute-start | bytes 221192 | tf_op jit(solution)/shard_map/ppermute | solution.py:441
  32.2 1.5 %collective-permute-start.8 = (bf16[512,256]{1,0:T(8,128)(2,1)S(1)}, bf16[512,256]{1,0:T(8,128)(2,1)S(1)}, u32[]{:S(2)}, u32[]{:S(2)}) collective-permute-start(bf16[512,256]{1,0:T(8,128)(2,1)S(1)} %column_sums.1.after.refs_0_), channel_id=1, source_target_pairs={{0,16},{8,24},{16,0},{24,8},{1,17},{9,25},{17,1},{25,9},{2,18},{10... | collective-permute-start | bytes 786440 | tf_op jit(solution)/shard_map/ppermute | solution.py:424
  33.8 1.5 %collective-permute-start.7 = (bf16[512,256]{1,0:T(8,128)(2,1)S(1)}, bf16[512,256]{1,0:T(8,128)(2,1)S(1)}, u32[]{:S(2)}, u32[]{:S(2)}) collective-permute-start(bf16[512,256]{1,0:T(8,128)(2,1)S(1)} %column_sums.1.after.refs_0_), channel_id=1, source_target_pairs={{0,8},{8,0},{16,24},{24,16},{1,9},{9,1},{17,25},{25,17},{2,10},{10... | collective-permute-start | bytes 786440 | tf_op jit(solution)/shard_map/ppermute | solution.py:424
  35.3 0.0 collective-permute-done.12
  35.3 3.1 %collective-permute-done.11 = bf16[8,4608]{1,0:T(8,128)(2,1)S(1)} collective-permute-done((bf16[8,4608]{1,0:T(8,128)(2,1)S(1)}, bf16[8,4608]{1,0:T(8,128)(2,1)S(1)}, u32[]{:S(2)}, u32[]{:S(2)}) %collective-permute-start.11) | collective-permute-done | bytes 73760 | tf_op jit(solution)/shard_map/ppermute | solution.py:441
  38.3 0.0 collective-permute-done.10
  38.4 0.0 copy-start.3
  38.4 0.1 collective-permute-start.13
  38.4 2.5 %collective-permute-start.9 = (bf16[512,256]{1,0:T(8,128)(2,1)S(1)}, bf16[512,256]{1,0:T(8,128)(2,1)S(1)}, u32[]{:S(2)}, u32[]{:S(2)}) collective-permute-start(bf16[512,256]{1,0:T(8,128)(2,1)S(1)} %column_sums.1.after.refs_0_), channel_id=1, source_target_pairs={{0,24},{8,16},{16,8},{24,0},{1,25},{9,17},{17,9},{25,1},{2,26},{10... | collective-permute-start | bytes 786440 | tf_op jit(solution)/shard_map/ppermute | solution.py:424
  41.0 2.2 %row_table.1.table = bf16[8,128,1024]{2,1,0:T(8,128)(2,1)S(1)} custom-call(s32[2]{0:T(128)S(1)} %pad_add_fusion.place, bf16[512,256]{1,0:T(8,128)(2,1)S(1)} %column_sums.1.after.refs_0_), custom_call_target="tpu_custom_call" | custom-call | flops 8388608 | bytes 2097152 | tf_op jit(solution)/shard_map/row_table/pallas_call | solution.py:425
  43.2 0.0 collective-permute-done.8.refs_2_
  43.2 0.0 collective-permute-done.7.refs_1_
  43.2 1.0 %partial_rows.1.partial = f32[512,1024]{1,0:T(8,128)S(1)} custom-call(bf16[8,128,1024]{2,1,0:T(8,128)(2,1)S(1)} %row_table.1.table, bf16[512,256]{1,0:T(8,128)(2,1)S(1)} %column_sums.1.after.refs_0_, bf16[512,256]{1,0:T(8,128)(2,1)S(1)} %collective-permute-done.7.refs_1_, bf16[512,256]{1,0:T(8,128)(2,1)S(1)} %collective-permute-done.8.refs_2_), custom_call_target="tpu_custom_call" | custom-call | flops 1073741824 | bytes 4194304 | tf_op jit(solution)/shard_map/partial_rows/pallas_call | solution.py:444
  44.2 3.9 %collective-permute-done.9.last = bf16[512,256]{1,0:T(8,128)(2,1)S(1)} collective-permute-done((bf16[512,256]{1,0:T(8,128)(2,1)S(1)}, bf16[512,256]{1,0:T(8,128)(2,1)S(1)}, u32[]{:S(2)}, u32[]{:S(2)}) %collective-permute-start.9) | collective-permute-done | bytes 262176 | tf_op jit(solution)/shard_map/ppermute | solution.py:424
  48.1 0.0 collective-permute-done.13.queries_other
  48.1 0.0 copy-done.3
  48.1 7.9 %degrid.1 = (f32[4,2,2048]{2,1,0:T(2,128)S(1)}, f32[4,2,2048]{2,1,0:T(2,128)S(1)}) custom-call(s32[2]{0:T(128)S(1)} %pad_add_fusion.place, s32[32]{0:T(128)S(1)} %copy-done.3, bf16[8,128,1024]{2,1,0:T(8,128)(2,1)S(1)} %row_table.1.table, f32[512,1024]{1,0:T(8,128)S(1)} %partial_rows.1.partial, bf16[512,256]{1,0:T(8,128)(2,1)S(1)} %collective-permute-done.9.last, ...), custom_call_target="tpu_custom_call" | custom-call | flops 8589934592 | bytes 4194304 | tf_op jit(solution)/shard_map/degrid/pallas_call | solution.py:353
  55.9 0.1 collective-permute-start.14
  56.0 1.2 %collective-permute-done.14 = f32[4,2,2048]{2,1,0:T(2,128)S(1)} collective-permute-done((f32[4,2,2048]{2,1,0:T(2,128)S(1)}, f32[4,2,2048]{2,1,0:T(2,128)S(1)}, u32[]{:S(2)}, u32[]{:S(2)}) %collective-permute-start.14) | collective-permute-done | bytes 65568 | tf_op jit(solution)/shard_map/ppermute | solution.py:459
  57.3 0.1 collective-permute-start.15
  57.4 0.1 collective-permute-start.17
  57.5 3.4 %collective-permute-start.16 = (f32[2,2048]{1,0:T(2,128)S(1)}, f32[2,2048]{1,0:T(2,128)S(1)}, u32[]{:S(2)}, u32[]{:S(2)}) collective-permute-start(f32[2,2048]{1,0:T(2,128)S(1)} %get-tuple-element.25), channel_id=1, source_target_pairs={{0,4},{1,5},{2,6},{3,7},{4,0},{5,1},{6,2},{7,3},{8,12},{9,13},{10,... | collective-permute-start | bytes 49160 | tf_op jit(solution)/shard_map/ppermute | solution.py:463
  60.9 0.2 collective-permute-done.15
  61.1 1.9 %collective-permute-done.17 = f32[2,2048]{1,0:T(2,128)S(1)} collective-permute-done((f32[2,2048]{1,0:T(2,128)S(1)}, f32[2,2048]{1,0:T(2,128)S(1)}, u32[]{:S(2)}, u32[]{:S(2)}) %collective-permute-start.17) | collective-permute-done | bytes 16416 | tf_op jit(solution)/shard_map/ppermute | solution.py:463
  63.0 0.0 collective-permute-done.16
  63.0 0.6 fusion.2
  (5 shorter events, 0.1 us)
Async XLA Ops:
  0.8 2.4 %slice-start = ((s8[8388608]{0:T(1024)(128)(4,1)}), s8[4194304]{0:T(1024)(128)(4,1)S(1)}, s32[]{:S(2)}) async-start(s8[8388608]{0:T(1024)(128)(4,1)} %bitcast.20), calls=%async_computation | async-start | bytes 8388608
  0.8 3.4 %slice-start.1 = ((s8[8388608]{0:T(1024)(128)(4,1)}), s8[4194304]{0:T(1024)(128)(4,1)S(1)}, s32[]{:S(2)}) async-start(s8[8388608]{0:T(1024)(128)(4,1)} %bitcast.20), calls=%async_computation.1 | async-start | bytes 8388608
  6.9 18.0 %collective-permute-start = (bf16[128,512]{1,0:T(8,128)(2,1)S(1)}, bf16[128,512]{1,0:T(8,128)(2,1)S(1)}, u32[]{:S(2)}, u32[]{:S(2)}) collective-permute-start(bf16[128,512]{1,0:T(8,128)(2,1)S(1)} %facet_blocks.5), channel_id=1, source_target_pairs={{0,4},{1,5},{2,6},{3,7},{4,0},{5,1},{6,2},{7,3},{8,12},{9,13},{10,... | collective-permute-start | bytes 393224 | tf_op jit(solution)/shard_map/ppermute | solution.py:399
  13.8 11.2 %collective-permute-start.1 = (bf16[128,512]{1,0:T(8,128)(2,1)S(1)}, bf16[128,512]{1,0:T(8,128)(2,1)S(1)}, u32[]{:S(2)}, u32[]{:S(2)}) collective-permute-start(bf16[128,512]{1,0:T(8,128)(2,1)S(1)} %facet_blocks.6), channel_id=1, source_target_pairs={{0,6},{1,7},{2,4},{3,5},{4,2},{5,3},{6,0},{7,1},{8,14},{9,15},{10,... | collective-permute-start | bytes 393224 | tf_op jit(solution)/shard_map/ppermute | solution.py:399
  20.4 5.7 %copy-start = (f32[8,2048]{1,0:T(8,128)S(1)}, f32[8,2048]{1,0:T(8,128)}, u32[]{:S(2)}) copy-start(f32[8,2048]{1,0:T(8,128)} %col_kernel.1) | copy-start | bytes 196612
  20.4 5.6 %copy-start.1 = (bf16[8,2048]{1,0:T(8,128)(2,1)S(1)}, bf16[8,2048]{1,0:T(8,128)(2,1)}, u32[]{:S(2)}) copy-start(bf16[8,2048]{1,0:T(8,128)(2,1)} %row_kernel.1) | copy-start | bytes 98308
  20.4 5.6 %copy-start.2 = (s32[2,2048]{1,0:T(2,128)S(1)}, s32[2,2048]{1,0:T(2,128)}, u32[]{:S(2)}) copy-start(s32[2,2048]{1,0:T(2,128)} %vis_cells.1) | copy-start | bytes 49156
  20.4 5.1 %collective-permute-start.2 = (bf16[128,512]{1,0:T(8,128)(2,1)S(1)}, bf16[128,512]{1,0:T(8,128)(2,1)S(1)}, u32[]{:S(2)}, u32[]{:S(2)}) collective-permute-start(bf16[128,512]{1,0:T(8,128)(2,1)S(1)} %facet_blocks.7), channel_id=1, source_target_pairs={{0,2},{1,3},{2,0},{3,1},{4,6},{5,7},{6,4},{7,5},{8,10},{9,11},{10,... | collective-permute-start | bytes 393224 | tf_op jit(solution)/shard_map/ppermute | solution.py:399
  23.4 2.6 %collective-permute-start.6 = (bf16[128,512]{1,0:T(8,128)(2,1)S(1)}, bf16[128,512]{1,0:T(8,128)(2,1)S(1)}, u32[]{:S(2)}, u32[]{:S(2)}) collective-permute-start(bf16[128,512]{1,0:T(8,128)(2,1)S(1)} %facet_blocks.4.after.refs_3_), channel_id=1, source_target_pairs={{0,1},{1,0},{2,3},{3,2},{4,5},{5,4},{6,7},{7,6},{8,9},{9,8},{10,11... | collective-permute-start | bytes 393224 | tf_op jit(solution)/shard_map/ppermute | solution.py:420
  25.0 1.9 %collective-permute-start.3 = (bf16[128,512]{1,0:T(8,128)(2,1)S(1)}, bf16[128,512]{1,0:T(8,128)(2,1)S(1)}, u32[]{:S(2)}, u32[]{:S(2)}) collective-permute-start(bf16[128,512]{1,0:T(8,128)(2,1)S(1)} %collective-permute-done.refs_0_), channel_id=1, source_target_pairs={{0,1},{1,0},{2,3},{3,2},{4,5},{5,4},{6,7},{7,6},{8,9},{9,8},{10,11... | collective-permute-start | bytes 393224 | tf_op jit(solution)/shard_map/ppermute | solution.py:420
  25.5 1.3 %collective-permute-start.5 = (bf16[128,512]{1,0:T(8,128)(2,1)S(1)}, bf16[128,512]{1,0:T(8,128)(2,1)S(1)}, u32[]{:S(2)}, u32[]{:S(2)}) collective-permute-start(bf16[128,512]{1,0:T(8,128)(2,1)S(1)} %collective-permute-done.2.refs_2_), channel_id=1, source_target_pairs={{0,1},{1,0},{2,3},{3,2},{4,5},{5,4},{6,7},{7,6},{8,9},{9,8},{10,11... | collective-permute-start | bytes 393224 | tf_op jit(solution)/shard_map/ppermute | solution.py:420
  25.6 1.4 %collective-permute-start.4 = (bf16[128,512]{1,0:T(8,128)(2,1)S(1)}, bf16[128,512]{1,0:T(8,128)(2,1)S(1)}, u32[]{:S(2)}, u32[]{:S(2)}) collective-permute-start(bf16[128,512]{1,0:T(8,128)(2,1)S(1)} %collective-permute-done.1.refs_1_), channel_id=1, source_target_pairs={{0,1},{1,0},{2,3},{3,2},{4,5},{5,4},{6,7},{7,6},{8,9},{9,8},{10,11... | collective-permute-start | bytes 393224 | tf_op jit(solution)/shard_map/ppermute | solution.py:420
  27.8 7.5 %collective-permute-start.12 = (bf16[8,4608]{1,0:T(8,128)(2,1)S(1)}, bf16[8,4608]{1,0:T(8,128)(2,1)S(1)}, u32[]{:S(2)}, u32[]{:S(2)}) collective-permute-start(bf16[8,4608]{1,0:T(8,128)(2,1)S(1)} %query.1), channel_id=1, source_target_pairs={{0,6},{1,7},{2,4},{3,5},{4,2},{5,3},{6,0},{7,1},{8,14},{9,15},{10,... | collective-permute-start | bytes 221192 | tf_op jit(solution)/shard_map/ppermute | solution.py:441
  30.8 7.5 %collective-permute-start.11 = (bf16[8,4608]{1,0:T(8,128)(2,1)S(1)}, bf16[8,4608]{1,0:T(8,128)(2,1)S(1)}, u32[]{:S(2)}, u32[]{:S(2)}) collective-permute-start(bf16[8,4608]{1,0:T(8,128)(2,1)S(1)} %query.1), channel_id=1, source_target_pairs={{0,4},{1,5},{2,6},{3,7},{4,0},{5,1},{6,2},{7,3},{8,12},{9,13},{10,... | collective-permute-start | bytes 221192 | tf_op jit(solution)/shard_map/ppermute | solution.py:441
  31.1 7.2 %collective-permute-start.10 = (bf16[8,4608]{1,0:T(8,128)(2,1)S(1)}, bf16[8,4608]{1,0:T(8,128)(2,1)S(1)}, u32[]{:S(2)}, u32[]{:S(2)}) collective-permute-start(bf16[8,4608]{1,0:T(8,128)(2,1)S(1)} %query.1), channel_id=1, source_target_pairs={{0,2},{1,3},{2,0},{3,1},{4,6},{5,7},{6,4},{7,5},{8,10},{9,11},{10,... | collective-permute-start | bytes 221192 | tf_op jit(solution)/shard_map/ppermute | solution.py:441
  32.2 10.9 %collective-permute-start.8 = (bf16[512,256]{1,0:T(8,128)(2,1)S(1)}, bf16[512,256]{1,0:T(8,128)(2,1)S(1)}, u32[]{:S(2)}, u32[]{:S(2)}) collective-permute-start(bf16[512,256]{1,0:T(8,128)(2,1)S(1)} %column_sums.1.after.refs_0_), channel_id=1, source_target_pairs={{0,16},{8,24},{16,0},{24,8},{1,17},{9,25},{17,1},{25,9},{2,18},{10... | collective-permute-start | bytes 786440 | tf_op jit(solution)/shard_map/ppermute | solution.py:424
  33.8 9.4 %collective-permute-start.7 = (bf16[512,256]{1,0:T(8,128)(2,1)S(1)}, bf16[512,256]{1,0:T(8,128)(2,1)S(1)}, u32[]{:S(2)}, u32[]{:S(2)}) collective-permute-start(bf16[512,256]{1,0:T(8,128)(2,1)S(1)} %column_sums.1.after.refs_0_), channel_id=1, source_target_pairs={{0,8},{8,0},{16,24},{24,16},{1,9},{9,1},{17,25},{25,17},{2,10},{10... | collective-permute-start | bytes 786440 | tf_op jit(solution)/shard_map/ppermute | solution.py:424
  38.4 9.7 %copy-start.3 = (s32[32]{0:T(128)S(1)}, s32[32]{0:T(128)}, u32[]{:S(2)}) copy-start(s32[32]{0:T(128)} %readers.1) | copy-start | bytes 388
  38.4 9.7 %collective-permute-start.13 = (bf16[4,8,4608]{2,1,0:T(8,128)(2,1)S(1)}, bf16[4,8,4608]{2,1,0:T(8,128)(2,1)S(1)}, u32[]{:S(2)}, u32[]{:S(2)}) collective-permute-start(bf16[4,8,4608]{2,1,0:T(8,128)(2,1)S(1)} %pad_maximum_fusion.queries_own), channel_id=1, source_target_pairs={{0,1},{1,0},{2,3},{3,2},{4,5},{5,4},{6,7},{7,6},{8,9},{9,8},{10,11... | collective-permute-start | bytes 884744 | tf_op jit(solution)/shard_map/ppermute | solution.py:443
  38.4 9.6 %collective-permute-start.9 = (bf16[512,256]{1,0:T(8,128)(2,1)S(1)}, bf16[512,256]{1,0:T(8,128)(2,1)S(1)}, u32[]{:S(2)}, u32[]{:S(2)}) collective-permute-start(bf16[512,256]{1,0:T(8,128)(2,1)S(1)} %column_sums.1.after.refs_0_), channel_id=1, source_target_pairs={{0,24},{8,16},{16,8},{24,0},{1,25},{9,17},{17,9},{25,1},{2,26},{10... | collective-permute-start | bytes 786440 | tf_op jit(solution)/shard_map/ppermute | solution.py:424
  55.9 1.3 %collective-permute-start.14 = (f32[4,2,2048]{2,1,0:T(2,128)S(1)}, f32[4,2,2048]{2,1,0:T(2,128)S(1)}, u32[]{:S(2)}, u32[]{:S(2)}) collective-permute-start(f32[4,2,2048]{2,1,0:T(2,128)S(1)} %get-tuple-element.22), channel_id=1, source_target_pairs={{0,1},{1,0},{2,3},{3,2},{4,5},{5,4},{6,7},{7,6},{8,9},{9,8},{10,11... | collective-permute-start | bytes 196616 | tf_op jit(solution)/shard_map/ppermute | solution.py:459
  57.3 3.8 %collective-permute-start.15 = (f32[2,2048]{1,0:T(2,128)S(1)}, f32[2,2048]{1,0:T(2,128)S(1)}, u32[]{:S(2)}, u32[]{:S(2)}) collective-permute-start(f32[2,2048]{1,0:T(2,128)S(1)} %get-tuple-element.23), channel_id=1, source_target_pairs={{0,2},{1,3},{2,0},{3,1},{4,6},{5,7},{6,4},{7,5},{8,10},{9,11},{10,... | collective-permute-start | bytes 49160 | tf_op jit(solution)/shard_map/ppermute | solution.py:463
  57.4 5.6 %collective-permute-start.17 = (f32[2,2048]{1,0:T(2,128)S(1)}, f32[2,2048]{1,0:T(2,128)S(1)}, u32[]{:S(2)}, u32[]{:S(2)}) collective-permute-start(f32[2,2048]{1,0:T(2,128)S(1)} %get-tuple-element.24), channel_id=1, source_target_pairs={{0,6},{1,7},{2,4},{3,5},{4,2},{5,3},{6,0},{7,1},{8,14},{9,15},{10,... | collective-permute-start | bytes 49160 | tf_op jit(solution)/shard_map/ppermute | solution.py:463
  57.5 5.5 %collective-permute-start.16 = (f32[2,2048]{1,0:T(2,128)S(1)}, f32[2,2048]{1,0:T(2,128)S(1)}, u32[]{:S(2)}, u32[]{:S(2)}) collective-permute-start(f32[2,2048]{1,0:T(2,128)S(1)} %get-tuple-element.25), channel_id=1, source_target_pairs={{0,4},{1,5},{2,6},{3,7},{4,0},{5,1},{6,2},{7,3},{8,12},{9,13},{10,... | collective-permute-start | bytes 49160 | tf_op jit(solution)/shard_map/ppermute | solution.py:463

commit v3 on v2

--- a/solution.py
+++ b/solution.py
@@ -389,9 +389,11 @@
 
     steps = [*range(2, NSUB), 1, 0]
     blocks = []
-    for start in range(0, NSUB, 2):
-        tables = strip_tables(meta, sky, steps[start : start + 2], (sky_cells, row_spacing, copies))
-        for at, step in enumerate(steps[start : start + 2]):
+    for group in (steps[:-1], steps[-1:]):
+        tables = strip_tables(
+            meta, sky, group, (sky_cells, row_spacing, copies)
+        )
+        for at, step in enumerate(group):
             block = facet_blocks(sky, tables, at)
             for copy_step in range(copies):
                 moved = block

time: 63.8 us -> 63.4 us (level)
  starting transfers between devices: 20.6 us -> 21.5 us
  local copies, waits for them, and re-layouts: 1.85 us -> 0.97 us
    ppermute x3, starting transfers between devices: 3.54 us -> 4.44 us  [local(): vis = vis + lax.ppermute(both[step], 'fy', ring)]
    unnamed x12, local copies, waits for them, and re-layouts: 1.09 us -> 0.21 us
  transfers between devices with their start and end apart: 18 -> 18, of which waited for: 7 -> 8; matrix products, arithmetic and copies ran while one was open for 0% -> 0% of each run, Pallas kernels for 24% -> 23%
where the time goes in v3:
time: 63.4 us; the launch traced here: 63.2 us
  Pallas kernels  28.7 us (45%)
  starting transfers between devices  21.5 us (34%)
  waiting for transfers between devices  10.9 us (17%)
  local copies, waits for them, and re-layouts  0.97 us (2%)
  other arithmetic  0.85 us (1%)
    pallas_call x4, Pallas kernels, facet_blocks(): pl.pallas_call(functools.partial(blocks_kernel, at), in_specs=[VMEM] * 3,...  10.8 us
    pallas_call x1, Pallas kernels, degrid(): pl.pallas_call(functools.partial(degrid_kernel, geometry), in_specs=[SMEM...  7.88 us
    ppermute x3, starting transfers between devices, local(): moved = lax.ppermute(block, 'fy', plane_shift(step, copy_step))  5.85 us
    ppermute x3, starting transfers between devices, local(): lax.ppermute(sums[0], 'fx', [(i, i ^ step) for i in range(rows_axis)])  5.52 us
    pallas_call x2, Pallas kernels, strip_tables(): pl.pallas_call(functools.partial(tables_kernel, steps, geometry), in_spec...  4.84 us
    ppermute x3, starting transfers between devices, local(): queries.append(lax.ppermute(moved, 'fy', ring))  4.45 us
    ppermute x3, starting transfers between devices, local(): vis = vis + lax.ppermute(both[step], 'fy', ring)  4.44 us
    ppermute x3, waiting for transfers between devices, local(): lax.ppermute(sums[0], 'fx', [(i, i ^ step) for i in range(rows_axis)])  3.86 us
  transfers between devices with their start and end apart: 18, of which 8 were waited for; matrix products, arithmetic and copies ran while one was open for 0% of the time, Pallas kernels for 23%

profile of v3, /device:TPU:0, one launch (start us, length us, event | category | flops | bytes accessed | tf_op | source)
XLA Modules:
  0.0 63.2 jit_solution(5385308574573566403)
XLA Ops:
  0.0 0.8 %reshape.3 = s32[8]{0:T(128)S(1)} reshape(s32[2,4]{1,0:T(2,128)} %param.7) | data formatting | bytes 64 | tf_op jit(solution)/shard_map/reshape | solution.py:379
  0.8 0.0 slice-start
  0.8 0.1 pad_add_fusion.1.meta
  0.8 0.0 slice-start.1
  0.8 3.2 %strip_tables.3 = (bf16[4096,768]{1,0:T(8,128)(2,1)S(1)}, bf16[6,512,256]{2,1,0:T(8,128)(2,1)S(1)}) custom-call(s32[10]{0:T(128)S(1)} %pad_add_fusion.1.meta), custom_call_target="tpu_custom_call" | custom-call | flops 8589934592 | bytes 16777216 | tf_op jit(solution)/shard_map/strip_tables/pallas_call | solution.py:141
  4.1 0.0 slice-done
  4.1 0.2 slice-done.1
  4.2 2.7 %facet_blocks.5 = bf16[128,512]{1,0:T(8,128)(2,1)S(1)} custom-call(bf16[1024,4096]{1,0:T(8,128)(2,1)S(1)} %bitcast.21, bf16[4096,768]{1,0:T(8,128)(2,1)S(1)} %get-tuple-element.16.cols, bf16[6,512,256]{2,1,0:T(8,128)(2,1)S(1)} %get-tuple-element.17.rows), custom_call_target="tpu_custom_call" | custom-call | flops 2147483648 | bytes 8388608 | tf_op jit(solution)/shard_map/facet_blocks/pallas_call | solution.py:178
  6.9 4.1 %collective-permute-start = (bf16[128,512]{1,0:T(8,128)(2,1)S(1)}, bf16[128,512]{1,0:T(8,128)(2,1)S(1)}, u32[]{:S(2)}, u32[]{:S(2)}) collective-permute-start(bf16[128,512]{1,0:T(8,128)(2,1)S(1)} %facet_blocks.5), channel_id=1, source_target_pairs={{0,4},{1,5},{2,6},{3,7},{4,0},{5,1},{6,2},{7,3},{8,12},{9,13},{10,... | collective-permute-start | bytes 393224 | tf_op jit(solution)/shard_map/ppermute | solution.py:401
  11.1 2.7 %facet_blocks.6 = bf16[128,512]{1,0:T(8,128)(2,1)S(1)} custom-call(bf16[1024,4096]{1,0:T(8,128)(2,1)S(1)} %bitcast.21, bf16[4096,768]{1,0:T(8,128)(2,1)S(1)} %get-tuple-element.16.cols, bf16[6,512,256]{2,1,0:T(8,128)(2,1)S(1)} %get-tuple-element.17.rows), custom_call_target="tpu_custom_call" | custom-call | flops 2147483648 | bytes 8388608 | tf_op jit(solution)/shard_map/facet_blocks/pallas_call | solution.py:178
  13.8 1.4 %collective-permute-start.1 = (bf16[128,512]{1,0:T(8,128)(2,1)S(1)}, bf16[128,512]{1,0:T(8,128)(2,1)S(1)}, u32[]{:S(2)}, u32[]{:S(2)}) collective-permute-start(bf16[128,512]{1,0:T(8,128)(2,1)S(1)} %facet_blocks.6), channel_id=1, source_target_pairs={{0,6},{1,7},{2,4},{3,5},{4,2},{5,3},{6,0},{7,1},{8,14},{9,15},{10,... | collective-permute-start | bytes 393224 | tf_op jit(solution)/shard_map/ppermute | solution.py:401
  15.2 2.7 %facet_blocks.7 = bf16[128,512]{1,0:T(8,128)(2,1)S(1)} custom-call(bf16[1024,4096]{1,0:T(8,128)(2,1)S(1)} %bitcast.21, bf16[4096,768]{1,0:T(8,128)(2,1)S(1)} %get-tuple-element.16.cols, bf16[6,512,256]{2,1,0:T(8,128)(2,1)S(1)} %get-tuple-element.17.rows), custom_call_target="tpu_custom_call" | custom-call | flops 2147483648 | bytes 8388608 | tf_op jit(solution)/shard_map/facet_blocks/pallas_call | solution.py:178
  17.9 0.3 collective-permute-start.2
  18.2 1.6 %strip_tables.2 = (bf16[4096,256]{1,0:T(8,128)(2,1)S(1)}, bf16[2,512,256]{2,1,0:T(8,128)(2,1)S(1)}) custom-call(s32[10]{0:T(128)S(1)} %pad_add_fusion.1.meta), custom_call_target="tpu_custom_call" | custom-call | flops 8589934592 | bytes 16777216 | tf_op jit(solution)/shard_map/strip_tables/pallas_call | solution.py:141
  19.8 0.0 copy-start
  19.8 0.0 copy-start.1
  19.8 0.0 copy-start.2
  19.9 2.7 %facet_blocks.4.after.refs_3_ = bf16[128,512]{1,0:T(8,128)(2,1)S(1)} custom-call(bf16[1024,4096]{1,0:T(8,128)(2,1)S(1)} %bitcast.21, bf16[4096,256]{1,0:T(8,128)(2,1)S(1)} %get-tuple-element.14.cols, bf16[2,512,256]{2,1,0:T(8,128)(2,1)S(1)} %get-tuple-element.15.rows), custom_call_target="tpu_custom_call" | custom-call | flops 2147483648 | bytes 8388608 | tf_op jit(solution)/shard_map/facet_blocks/pallas_call | solution.py:178
  22.6 0.1 collective-permute-start.6
  22.6 0.1 pad_add_fusion.place
  22.7 1.4 %col_table.1.table = bf16[8,512,128]{2,1,0:T(8,128)(2,1)S(1)} custom-call(s32[2]{0:T(128)S(1)} %pad_add_fusion.place, bf16[128,512]{1,0:T(8,128)(2,1)S(1)} %facet_blocks.4.after.refs_3_), custom_call_target="tpu_custom_call" | custom-call | flops 4194304 | bytes 1048576 | tf_op jit(solution)/shard_map/col_table/pallas_call | solution.py:404
  24.1 0.0 collective-permute-done.refs_0_
  24.1 0.0 collective-permute-done.1.refs_1_
  24.1 0.6 collective-permute-start.3
  24.6 0.1 collective-permute-start.4
  24.7 0.0 collective-permute-done.2.refs_2_
  24.7 0.4 collective-permute-start.5
  25.2 0.0 copy-done
  25.2 0.0 copy-done.1
  25.2 0.0 copy-done.2
  25.2 0.0 collective-permute-done.6.refs_7_
  25.2 0.4 collective-permute-done.3.refs_4_
  25.6 0.4 collective-permute-done.4.refs_5_
  26.0 0.2 collective-permute-done.5.refs_6_
  26.2 0.7 %column_sums.1.after.refs_0_ = bf16[512,256]{1,0:T(8,128)(2,1)S(1)} custom-call(bf16[8,512,128]{2,1,0:T(8,128)(2,1)S(1)} %col_table.1.table, bf16[128,512]{1,0:T(8,128)(2,1)S(1)} %collective-permute-done.refs_0_, bf16[128,512]{1,0:T(8,128)(2,1)S(1)} %collective-permute-done.1.refs_1_, bf16[128,512]{1,0:T(8,128)(2,1)S(1)} %collective-permute-done.2.refs_2_, ...), custom_call_target="tpu_custom_call" | custom-call | flops 536870912 | bytes 2097152 | tf_op jit(solution)/shard_map/column_sums/pallas_call | solution.py:252
  26.9 3.0 %collective-permute-start.12 = (bf16[8,4608]{1,0:T(8,128)(2,1)S(1)}, bf16[8,4608]{1,0:T(8,128)(2,1)S(1)}, u32[]{:S(2)}, u32[]{:S(2)}) collective-permute-start(bf16[8,4608]{1,0:T(8,128)(2,1)S(1)} %query.1), channel_id=1, source_target_pairs={{0,6},{1,7},{2,4},{3,5},{4,2},{5,3},{6,0},{7,1},{8,14},{9,15},{10,... | collective-permute-start | bytes 221192 | tf_op jit(solution)/shard_map/ppermute | solution.py:443
  29.9 0.3 collective-permute-start.11
  30.2 1.1 %collective-permute-start.10 = (bf16[8,4608]{1,0:T(8,128)(2,1)S(1)}, bf16[8,4608]{1,0:T(8,128)(2,1)S(1)}, u32[]{:S(2)}, u32[]{:S(2)}) collective-permute-start(bf16[8,4608]{1,0:T(8,128)(2,1)S(1)} %query.1), channel_id=1, source_target_pairs={{0,2},{1,3},{2,0},{3,1},{4,6},{5,7},{6,4},{7,5},{8,10},{9,11},{10,... | collective-permute-start | bytes 221192 | tf_op jit(solution)/shard_map/ppermute | solution.py:443
  31.4 1.5 %collective-permute-start.7 = (bf16[512,256]{1,0:T(8,128)(2,1)S(1)}, bf16[512,256]{1,0:T(8,128)(2,1)S(1)}, u32[]{:S(2)}, u32[]{:S(2)}) collective-permute-start(bf16[512,256]{1,0:T(8,128)(2,1)S(1)} %column_sums.1.after.refs_0_), channel_id=1, source_target_pairs={{0,8},{8,0},{16,24},{24,16},{1,9},{9,1},{17,25},{25,17},{2,10},{10... | collective-permute-start | bytes 786440 | tf_op jit(solution)/shard_map/ppermute | solution.py:426
  32.8 1.5 %collective-permute-start.8 = (bf16[512,256]{1,0:T(8,128)(2,1)S(1)}, bf16[512,256]{1,0:T(8,128)(2,1)S(1)}, u32[]{:S(2)}, u32[]{:S(2)}) collective-permute-start(bf16[512,256]{1,0:T(8,128)(2,1)S(1)} %column_sums.1.after.refs_0_), channel_id=1, source_target_pairs={{0,16},{8,24},{16,0},{24,8},{1,17},{9,25},{17,1},{25,9},{2,18},{10... | collective-permute-start | bytes 786440 | tf_op jit(solution)/shard_map/ppermute | solution.py:426
  34.4 0.0 collective-permute-done.12
  34.4 3.1 %collective-permute-done.11 = bf16[8,4608]{1,0:T(8,128)(2,1)S(1)} collective-permute-done((bf16[8,4608]{1,0:T(8,128)(2,1)S(1)}, bf16[8,4608]{1,0:T(8,128)(2,1)S(1)}, u32[]{:S(2)}, u32[]{:S(2)}) %collective-permute-start.11) | collective-permute-done | bytes 73760 | tf_op jit(solution)/shard_map/ppermute | solution.py:443
  37.4 0.0 collective-permute-done.10
  37.5 0.1 collective-permute-start.13
  37.5 2.5 %collective-permute-start.9 = (bf16[512,256]{1,0:T(8,128)(2,1)S(1)}, bf16[512,256]{1,0:T(8,128)(2,1)S(1)}, u32[]{:S(2)}, u32[]{:S(2)}) collective-permute-start(bf16[512,256]{1,0:T(8,128)(2,1)S(1)} %column_sums.1.after.refs_0_), channel_id=1, source_target_pairs={{0,24},{8,16},{16,8},{24,0},{1,25},{9,17},{17,9},{25,1},{2,26},{10... | collective-permute-start | bytes 786440 | tf_op jit(solution)/shard_map/ppermute | solution.py:426
  40.1 2.2 %row_table.1.table = bf16[8,128,1024]{2,1,0:T(8,128)(2,1)S(1)} custom-call(s32[2]{0:T(128)S(1)} %pad_add_fusion.place, bf16[512,256]{1,0:T(8,128)(2,1)S(1)} %column_sums.1.after.refs_0_), custom_call_target="tpu_custom_call" | custom-call | flops 8388608 | bytes 2097152 | tf_op jit(solution)/shard_map/row_table/pallas_call | solution.py:427
  42.3 0.0 copy-start.3
  42.3 0.0 collective-permute-done.7.refs_1_
  42.3 0.0 collective-permute-done.8.refs_2_
  42.3 1.0 %partial_rows.1.partial = f32[512,1024]{1,0:T(8,128)S(1)} custom-call(bf16[8,128,1024]{2,1,0:T(8,128)(2,1)S(1)} %row_table.1.table, bf16[512,256]{1,0:T(8,128)(2,1)S(1)} %column_sums.1.after.refs_0_, bf16[512,256]{1,0:T(8,128)(2,1)S(1)} %collective-permute-done.7.refs_1_, bf16[512,256]{1,0:T(8,128)(2,1)S(1)} %collective-permute-done.8.refs_2_), custom_call_target="tpu_custom_call" | custom-call | flops 1073741824 | bytes 4194304 | tf_op jit(solution)/shard_map/partial_rows/pallas_call | solution.py:446
  43.3 3.9 %collective-permute-done.9.last = bf16[512,256]{1,0:T(8,128)(2,1)S(1)} collective-permute-done((bf16[512,256]{1,0:T(8,128)(2,1)S(1)}, bf16[512,256]{1,0:T(8,128)(2,1)S(1)}, u32[]{:S(2)}, u32[]{:S(2)}) %collective-permute-start.9) | collective-permute-done | bytes 262176 | tf_op jit(solution)/shard_map/ppermute | solution.py:426
  47.2 0.0 collective-permute-done.13.queries_other
  47.2 0.0 copy-done.3
  47.2 7.9 %degrid.1 = (f32[4,2,2048]{2,1,0:T(2,128)S(1)}, f32[4,2,2048]{2,1,0:T(2,128)S(1)}) custom-call(s32[2]{0:T(128)S(1)} %pad_add_fusion.place, s32[32]{0:T(128)S(1)} %copy-done.3, bf16[8,128,1024]{2,1,0:T(8,128)(2,1)S(1)} %row_table.1.table, f32[512,1024]{1,0:T(8,128)S(1)} %partial_rows.1.partial, bf16[512,256]{1,0:T(8,128)(2,1)S(1)} %collective-permute-done.9.last, ...), custom_call_target="tpu_custom_call" | custom-call | flops 8589934592 | bytes 4194304 | tf_op jit(solution)/shard_map/degrid/pallas_call | solution.py:353
  55.0 0.1 collective-permute-start.14
  55.1 1.2 %collective-permute-done.14 = f32[4,2,2048]{2,1,0:T(2,128)S(1)} collective-permute-done((f32[4,2,2048]{2,1,0:T(2,128)S(1)}, f32[4,2,2048]{2,1,0:T(2,128)S(1)}, u32[]{:S(2)}, u32[]{:S(2)}) %collective-permute-start.14) | collective-permute-done | bytes 65568 | tf_op jit(solution)/shard_map/ppermute | solution.py:461
  56.4 0.1 collective-permute-start.17
  56.5 0.1 collective-permute-start.16
  56.6 4.3 %collective-permute-start.15 = (f32[2,2048]{1,0:T(2,128)S(1)}, f32[2,2048]{1,0:T(2,128)S(1)}, u32[]{:S(2)}, u32[]{:S(2)}) collective-permute-start(f32[2,2048]{1,0:T(2,128)S(1)} %get-tuple-element.23), channel_id=1, source_target_pairs={{0,2},{1,3},{2,0},{3,1},{4,6},{5,7},{6,4},{7,5},{8,10},{9,11},{10,... | collective-permute-start | bytes 49160 | tf_op jit(solution)/shard_map/ppermute | solution.py:465
  60.9 1.1 %collective-permute-done.17 = f32[2,2048]{1,0:T(2,128)S(1)} collective-permute-done((f32[2,2048]{1,0:T(2,128)S(1)}, f32[2,2048]{1,0:T(2,128)S(1)}, u32[]{:S(2)}, u32[]{:S(2)}) %collective-permute-start.17) | collective-permute-done | bytes 16416 | tf_op jit(solution)/shard_map/ppermute | solution.py:465
  62.0 0.0 collective-permute-done.16
  62.0 0.6 collective-permute-done.15
  62.6 0.6 fusion.2
  (5 shorter events, 0.1 us)
Async XLA Ops:
  0.8 3.3 %slice-start = ((s8[8388608]{0:T(1024)(128)(4,1)}), s8[4194304]{0:T(1024)(128)(4,1)S(1)}, s32[]{:S(2)}) async-start(s8[8388608]{0:T(1024)(128)(4,1)} %bitcast.20), calls=%async_computation | async-start | bytes 8388608
  0.8 3.4 %slice-start.1 = ((s8[8388608]{0:T(1024)(128)(4,1)}), s8[4194304]{0:T(1024)(128)(4,1)S(1)}, s32[]{:S(2)}) async-start(s8[8388608]{0:T(1024)(128)(4,1)} %bitcast.20), calls=%async_computation.1 | async-start | bytes 8388608
  6.9 17.1 %collective-permute-start = (bf16[128,512]{1,0:T(8,128)(2,1)S(1)}, bf16[128,512]{1,0:T(8,128)(2,1)S(1)}, u32[]{:S(2)}, u32[]{:S(2)}) collective-permute-start(bf16[128,512]{1,0:T(8,128)(2,1)S(1)} %facet_blocks.5), channel_id=1, source_target_pairs={{0,4},{1,5},{2,6},{3,7},{4,0},{5,1},{6,2},{7,3},{8,12},{9,13},{10,... | collective-permute-start | bytes 393224 | tf_op jit(solution)/shard_map/ppermute | solution.py:401
  13.8 10.3 %collective-permute-start.1 = (bf16[128,512]{1,0:T(8,128)(2,1)S(1)}, bf16[128,512]{1,0:T(8,128)(2,1)S(1)}, u32[]{:S(2)}, u32[]{:S(2)}) collective-permute-start(bf16[128,512]{1,0:T(8,128)(2,1)S(1)} %facet_blocks.6), channel_id=1, source_target_pairs={{0,6},{1,7},{2,4},{3,5},{4,2},{5,3},{6,0},{7,1},{8,14},{9,15},{10,... | collective-permute-start | bytes 393224 | tf_op jit(solution)/shard_map/ppermute | solution.py:401
  17.9 6.9 %collective-permute-start.2 = (bf16[128,512]{1,0:T(8,128)(2,1)S(1)}, bf16[128,512]{1,0:T(8,128)(2,1)S(1)}, u32[]{:S(2)}, u32[]{:S(2)}) collective-permute-start(bf16[128,512]{1,0:T(8,128)(2,1)S(1)} %facet_blocks.7), channel_id=1, source_target_pairs={{0,2},{1,3},{2,0},{3,1},{4,6},{5,7},{6,4},{7,5},{8,10},{9,11},{10,... | collective-permute-start | bytes 393224 | tf_op jit(solution)/shard_map/ppermute | solution.py:401
  19.8 5.3 %copy-start = (f32[8,2048]{1,0:T(8,128)S(1)}, f32[8,2048]{1,0:T(8,128)}, u32[]{:S(2)}) copy-start(f32[8,2048]{1,0:T(8,128)} %col_kernel.1) | copy-start | bytes 196612
  19.8 5.3 %copy-start.1 = (bf16[8,2048]{1,0:T(8,128)(2,1)S(1)}, bf16[8,2048]{1,0:T(8,128)(2,1)}, u32[]{:S(2)}) copy-start(bf16[8,2048]{1,0:T(8,128)(2,1)} %row_kernel.1) | copy-start | bytes 98308
  19.8 5.3 %copy-start.2 = (s32[2,2048]{1,0:T(2,128)S(1)}, s32[2,2048]{1,0:T(2,128)}, u32[]{:S(2)}) copy-start(s32[2,2048]{1,0:T(2,128)} %vis_cells.1) | copy-start | bytes 49156
  22.6 2.6 %collective-permute-start.6 = (bf16[128,512]{1,0:T(8,128)(2,1)S(1)}, bf16[128,512]{1,0:T(8,128)(2,1)S(1)}, u32[]{:S(2)}, u32[]{:S(2)}) collective-permute-start(bf16[128,512]{1,0:T(8,128)(2,1)S(1)} %facet_blocks.4.after.refs_3_), channel_id=1, source_target_pairs={{0,1},{1,0},{2,3},{3,2},{4,5},{5,4},{6,7},{7,6},{8,9},{9,8},{10,11... | collective-permute-start | bytes 393224 | tf_op jit(solution)/shard_map/ppermute | solution.py:422
  24.1 1.5 %collective-permute-start.3 = (bf16[128,512]{1,0:T(8,128)(2,1)S(1)}, bf16[128,512]{1,0:T(8,128)(2,1)S(1)}, u32[]{:S(2)}, u32[]{:S(2)}) collective-permute-start(bf16[128,512]{1,0:T(8,128)(2,1)S(1)} %collective-permute-done.refs_0_), channel_id=1, source_target_pairs={{0,1},{1,0},{2,3},{3,2},{4,5},{5,4},{6,7},{7,6},{8,9},{9,8},{10,11... | collective-permute-start | bytes 393224 | tf_op jit(solution)/shard_map/ppermute | solution.py:422
  24.6 1.3 %collective-permute-start.4 = (bf16[128,512]{1,0:T(8,128)(2,1)S(1)}, bf16[128,512]{1,0:T(8,128)(2,1)S(1)}, u32[]{:S(2)}, u32[]{:S(2)}) collective-permute-start(bf16[128,512]{1,0:T(8,128)(2,1)S(1)} %collective-permute-done.1.refs_1_), channel_id=1, source_target_pairs={{0,1},{1,0},{2,3},{3,2},{4,5},{5,4},{6,7},{7,6},{8,9},{9,8},{10,11... | collective-permute-start | bytes 393224 | tf_op jit(solution)/shard_map/ppermute | solution.py:422
  24.7 1.5 %collective-permute-start.5 = (bf16[128,512]{1,0:T(8,128)(2,1)S(1)}, bf16[128,512]{1,0:T(8,128)(2,1)S(1)}, u32[]{:S(2)}, u32[]{:S(2)}) collective-permute-start(bf16[128,512]{1,0:T(8,128)(2,1)S(1)} %collective-permute-done.2.refs_2_), channel_id=1, source_target_pairs={{0,1},{1,0},{2,3},{3,2},{4,5},{5,4},{6,7},{7,6},{8,9},{9,8},{10,11... | collective-permute-start | bytes 393224 | tf_op jit(solution)/shard_map/ppermute | solution.py:422
  26.9 7.5 %collective-permute-start.12 = (bf16[8,4608]{1,0:T(8,128)(2,1)S(1)}, bf16[8,4608]{1,0:T(8,128)(2,1)S(1)}, u32[]{:S(2)}, u32[]{:S(2)}) collective-permute-start(bf16[8,4608]{1,0:T(8,128)(2,1)S(1)} %query.1), channel_id=1, source_target_pairs={{0,6},{1,7},{2,4},{3,5},{4,2},{5,3},{6,0},{7,1},{8,14},{9,15},{10,... | collective-permute-start | bytes 221192 | tf_op jit(solution)/shard_map/ppermute | solution.py:443
  29.9 7.6 %collective-permute-start.11 = (bf16[8,4608]{1,0:T(8,128)(2,1)S(1)}, bf16[8,4608]{1,0:T(8,128)(2,1)S(1)}, u32[]{:S(2)}, u32[]{:S(2)}) collective-permute-start(bf16[8,4608]{1,0:T(8,128)(2,1)S(1)} %query.1), channel_id=1, source_target_pairs={{0,4},{1,5},{2,6},{3,7},{4,0},{5,1},{6,2},{7,3},{8,12},{9,13},{10,... | collective-permute-start | bytes 221192 | tf_op jit(solution)/shard_map/ppermute | solution.py:443
  30.2 7.2 %collective-permute-start.10 = (bf16[8,4608]{1,0:T(8,128)(2,1)S(1)}, bf16[8,4608]{1,0:T(8,128)(2,1)S(1)}, u32[]{:S(2)}, u32[]{:S(2)}) collective-permute-start(bf16[8,4608]{1,0:T(8,128)(2,1)S(1)} %query.1), channel_id=1, source_target_pairs={{0,2},{1,3},{2,0},{3,1},{4,6},{5,7},{6,4},{7,5},{8,10},{9,11},{10,... | collective-permute-start | bytes 221192 | tf_op jit(solution)/shard_map/ppermute | solution.py:443
  31.4 10.9 %collective-permute-start.7 = (bf16[512,256]{1,0:T(8,128)(2,1)S(1)}, bf16[512,256]{1,0:T(8,128)(2,1)S(1)}, u32[]{:S(2)}, u32[]{:S(2)}) collective-permute-start(bf16[512,256]{1,0:T(8,128)(2,1)S(1)} %column_sums.1.after.refs_0_), channel_id=1, source_target_pairs={{0,8},{8,0},{16,24},{24,16},{1,9},{9,1},{17,25},{25,17},{2,10},{10... | collective-permute-start | bytes 786440 | tf_op jit(solution)/shard_map/ppermute | solution.py:426
  32.8 9.5 %collective-permute-start.8 = (bf16[512,256]{1,0:T(8,128)(2,1)S(1)}, bf16[512,256]{1,0:T(8,128)(2,1)S(1)}, u32[]{:S(2)}, u32[]{:S(2)}) collective-permute-start(bf16[512,256]{1,0:T(8,128)(2,1)S(1)} %column_sums.1.after.refs_0_), channel_id=1, source_target_pairs={{0,16},{8,24},{16,0},{24,8},{1,17},{9,25},{17,1},{25,9},{2,18},{10... | collective-permute-start | bytes 786440 | tf_op jit(solution)/shard_map/ppermute | solution.py:426
  37.5 9.7 %collective-permute-start.13 = (bf16[4,8,4608]{2,1,0:T(8,128)(2,1)S(1)}, bf16[4,8,4608]{2,1,0:T(8,128)(2,1)S(1)}, u32[]{:S(2)}, u32[]{:S(2)}) collective-permute-start(bf16[4,8,4608]{2,1,0:T(8,128)(2,1)S(1)} %pad_maximum_fusion.queries_own), channel_id=1, source_target_pairs={{0,1},{1,0},{2,3},{3,2},{4,5},{5,4},{6,7},{7,6},{8,9},{9,8},{10,11... | collective-permute-start | bytes 884744 | tf_op jit(solution)/shard_map/ppermute | solution.py:445
  37.5 9.6 %collective-permute-start.9 = (bf16[512,256]{1,0:T(8,128)(2,1)S(1)}, bf16[512,256]{1,0:T(8,128)(2,1)S(1)}, u32[]{:S(2)}, u32[]{:S(2)}) collective-permute-start(bf16[512,256]{1,0:T(8,128)(2,1)S(1)} %column_sums.1.after.refs_0_), channel_id=1, source_target_pairs={{0,24},{8,16},{16,8},{24,0},{1,25},{9,17},{17,9},{25,1},{2,26},{10... | collective-permute-start | bytes 786440 | tf_op jit(solution)/shard_map/ppermute | solution.py:426
  42.3 4.9 %copy-start.3 = (s32[32]{0:T(128)S(1)}, s32[32]{0:T(128)}, u32[]{:S(2)}) copy-start(s32[32]{0:T(128)} %readers.1) | copy-start | bytes 388
  55.0 1.3 %collective-permute-start.14 = (f32[4,2,2048]{2,1,0:T(2,128)S(1)}, f32[4,2,2048]{2,1,0:T(2,128)S(1)}, u32[]{:S(2)}, u32[]{:S(2)}) collective-permute-start(f32[4,2,2048]{2,1,0:T(2,128)S(1)} %get-tuple-element.22), channel_id=1, source_target_pairs={{0,1},{1,0},{2,3},{3,2},{4,5},{5,4},{6,7},{7,6},{8,9},{9,8},{10,11... | collective-permute-start | bytes 196616 | tf_op jit(solution)/shard_map/ppermute | solution.py:461
  56.4 5.6 %collective-permute-start.17 = (f32[2,2048]{1,0:T(2,128)S(1)}, f32[2,2048]{1,0:T(2,128)S(1)}, u32[]{:S(2)}, u32[]{:S(2)}) collective-permute-start(f32[2,2048]{1,0:T(2,128)S(1)} %get-tuple-element.24), channel_id=1, source_target_pairs={{0,6},{1,7},{2,4},{3,5},{4,2},{5,3},{6,0},{7,1},{8,14},{9,15},{10,... | collective-permute-start | bytes 49160 | tf_op jit(solution)/shard_map/ppermute | solution.py:465
  56.5 5.5 %collective-permute-start.16 = (f32[2,2048]{1,0:T(2,128)S(1)}, f32[2,2048]{1,0:T(2,128)S(1)}, u32[]{:S(2)}, u32[]{:S(2)}) collective-permute-start(f32[2,2048]{1,0:T(2,128)S(1)} %get-tuple-element.25), channel_id=1, source_target_pairs={{0,4},{1,5},{2,6},{3,7},{4,0},{5,1},{6,2},{7,3},{8,12},{9,13},{10,... | collective-permute-start | bytes 49160 | tf_op jit(solution)/shard_map/ppermute | solution.py:465
  56.6 6.0 %collective-permute-start.15 = (f32[2,2048]{1,0:T(2,128)S(1)}, f32[2,2048]{1,0:T(2,128)S(1)}, u32[]{:S(2)}, u32[]{:S(2)}) collective-permute-start(f32[2,2048]{1,0:T(2,128)S(1)} %get-tuple-element.23), channel_id=1, source_target_pairs={{0,2},{1,3},{2,0},{3,1},{4,6},{5,7},{6,4},{7,5},{8,10},{9,11},{10,... | collective-permute-start | bytes 49160 | tf_op jit(solution)/shard_map/ppermute | solution.py:465

commit v4 on v2

--- a/solution.py
+++ b/solution.py
@@ -389,15 +389,14 @@
 
     steps = [*range(2, NSUB), 1, 0]
     blocks = []
-    for start in range(0, NSUB, 2):
-        tables = strip_tables(meta, sky, steps[start : start + 2], (sky_cells, row_spacing, copies))
-        for at, step in enumerate(steps[start : start + 2]):
-            block = facet_blocks(sky, tables, at)
-            for copy_step in range(copies):
-                moved = block
-                if step or copy_step:
-                    moved = lax.ppermute(block, "fy", plane_shift(step, copy_step))
-                blocks.append(moved)
+    tables = strip_tables(meta, sky, steps, (sky_cells, row_spacing, copies))
+    for at, step in enumerate(steps):
+        block = facet_blocks(sky, tables, at)
+        for copy_step in range(copies):
+            moved = block
+            if step or copy_step:
+                moved = lax.ppermute(block, "fy", plane_shift(step, copy_step))
+            blocks.append(moved)
 
     col_table = pl.pallas_call(
         functools.partial(col_table_kernel, (sky_cells, copies, steps), factor),

time: 63.8 us -> 62.3 us (0.976)
  local copies, waits for them, and re-layouts: 1.85 us -> 0.8 us
    unnamed x12, local copies, waits for them, and re-layouts: 1.09 us -> 0.03 us
    pallas_call x2 -> x1, Pallas kernels: 4.84 us -> 4.41 us  [strip_tables(): pl.pallas_call(functools.partial(tables_kernel, steps, geometry), in_spec...]
  transfers between devices with their start and end apart: 18 -> 18, of which waited for: 7 -> 8; matrix products, arithmetic and copies ran while one was open for 0% -> 0% of each run, Pallas kernels for 24% -> 21%
where the time goes in v4:
time: 62.3 us; the launch traced here: 62.1 us
  Pallas kernels  28.5 us (46%)
  starting transfers between devices  20.7 us (33%)
  waiting for transfers between devices  11.1 us (18%)
  other arithmetic  0.85 us (1%)
  local copies, waits for them, and re-layouts  0.8 us (1%)
    pallas_call x4, Pallas kernels, facet_blocks(): pl.pallas_call(functools.partial(blocks_kernel, at), in_specs=[VMEM] * 3,...  10.8 us
    pallas_call x1, Pallas kernels, degrid(): pl.pallas_call(functools.partial(degrid_kernel, geometry), in_specs=[SMEM...  7.88 us
    ppermute x3, starting transfers between devices, local(): moved = lax.ppermute(block, 'fy', plane_shift(step, copy_step))  5.87 us
    ppermute x3, starting transfers between devices, local(): lax.ppermute(sums[0], 'fx', [(i, i ^ step) for i in range(rows_axis)])  5.52 us
    ppermute x3, starting transfers between devices, local(): queries.append(lax.ppermute(moved, 'fy', ring))  4.45 us
    pallas_call x1, Pallas kernels, strip_tables(): pl.pallas_call(functools.partial(tables_kernel, steps, geometry), in_spec...  4.41 us
    ppermute x3, waiting for transfers between devices, local(): lax.ppermute(sums[0], 'fx', [(i, i ^ step) for i in range(rows_axis)])  3.68 us
    ppermute x3, starting transfers between devices, local(): vis = vis + lax.ppermute(both[step], 'fy', ring)  3.54 us
  transfers between devices with their start and end apart: 18, of which 8 were waited for; matrix products, arithmetic and copies ran while one was open for 0% of the time, Pallas kernels for 21%

profile of v4, /device:TPU:0, one launch (start us, length us, event | category | flops | bytes accessed | tf_op | source)
XLA Modules:
  0.0 62.1 jit_solution(7600601422947456569)
XLA Ops:
  0.0 0.8 %reshape.3 = s32[8]{0:T(128)S(1)} reshape(s32[2,4]{1,0:T(2,128)} %param.7) | data formatting | bytes 64 | tf_op jit(solution)/shard_map/reshape | solution.py:379
  0.8 0.0 slice-start
  0.8 0.1 pad_add_fusion.1.meta
  0.8 0.0 slice-start.1
  0.8 4.4 %strip_tables.1 = (bf16[4096,1024]{1,0:T(8,128)(2,1)S(1)}, bf16[8,512,256]{2,1,0:T(8,128)(2,1)S(1)}) custom-call(s32[10]{0:T(128)S(1)} %pad_add_fusion.1.meta), custom_call_target="tpu_custom_call" | custom-call | flops 8589934592 | bytes 16777216 | tf_op jit(solution)/shard_map/strip_tables/pallas_call | solution.py:141
  5.3 0.0 slice-done
  5.3 0.0 slice-done.1
  5.3 2.7 %facet_blocks.5 = bf16[128,512]{1,0:T(8,128)(2,1)S(1)} custom-call(bf16[1024,4096]{1,0:T(8,128)(2,1)S(1)} %bitcast.21, bf16[4096,1024]{1,0:T(8,128)(2,1)S(1)} %get-tuple-element.12.cols, bf16[8,512,256]{2,1,0:T(8,128)(2,1)S(1)} %get-tuple-element.13.rows), custom_call_target="tpu_custom_call" | custom-call | flops 2147483648 | bytes 8388608 | tf_op jit(solution)/shard_map/facet_blocks/pallas_call | solution.py:178
  8.0 4.1 %collective-permute-start = (bf16[128,512]{1,0:T(8,128)(2,1)S(1)}, bf16[128,512]{1,0:T(8,128)(2,1)S(1)}, u32[]{:S(2)}, u32[]{:S(2)}) collective-permute-start(bf16[128,512]{1,0:T(8,128)(2,1)S(1)} %facet_blocks.5), channel_id=1, source_target_pairs={{0,4},{1,5},{2,6},{3,7},{4,0},{5,1},{6,2},{7,3},{8,12},{9,13},{10,... | collective-permute-start | bytes 393224 | tf_op jit(solution)/shard_map/ppermute | solution.py:398
  12.1 2.7 %facet_blocks.6 = bf16[128,512]{1,0:T(8,128)(2,1)S(1)} custom-call(bf16[1024,4096]{1,0:T(8,128)(2,1)S(1)} %bitcast.21, bf16[4096,1024]{1,0:T(8,128)(2,1)S(1)} %get-tuple-element.12.cols, bf16[8,512,256]{2,1,0:T(8,128)(2,1)S(1)} %get-tuple-element.13.rows), custom_call_target="tpu_custom_call" | custom-call | flops 2147483648 | bytes 8388608 | tf_op jit(solution)/shard_map/facet_blocks/pallas_call | solution.py:178
  14.8 1.4 %collective-permute-start.1 = (bf16[128,512]{1,0:T(8,128)(2,1)S(1)}, bf16[128,512]{1,0:T(8,128)(2,1)S(1)}, u32[]{:S(2)}, u32[]{:S(2)}) collective-permute-start(bf16[128,512]{1,0:T(8,128)(2,1)S(1)} %facet_blocks.6), channel_id=1, source_target_pairs={{0,6},{1,7},{2,4},{3,5},{4,2},{5,3},{6,0},{7,1},{8,14},{9,15},{10,... | collective-permute-start | bytes 393224 | tf_op jit(solution)/shard_map/ppermute | solution.py:398
  16.2 2.7 %facet_blocks.7 = bf16[128,512]{1,0:T(8,128)(2,1)S(1)} custom-call(bf16[1024,4096]{1,0:T(8,128)(2,1)S(1)} %bitcast.21, bf16[4096,1024]{1,0:T(8,128)(2,1)S(1)} %get-tuple-element.12.cols, bf16[8,512,256]{2,1,0:T(8,128)(2,1)S(1)} %get-tuple-element.13.rows), custom_call_target="tpu_custom_call" | custom-call | flops 2147483648 | bytes 8388608 | tf_op jit(solution)/shard_map/facet_blocks/pallas_call | solution.py:178
  18.9 0.0 copy-start
  18.9 0.0 copy-start.1
  18.9 0.0 copy-start.2
  19.0 0.3 collective-permute-start.2
  19.3 2.7 %facet_blocks.4.after.refs_3_ = bf16[128,512]{1,0:T(8,128)(2,1)S(1)} custom-call(bf16[1024,4096]{1,0:T(8,128)(2,1)S(1)} %bitcast.21, bf16[4096,1024]{1,0:T(8,128)(2,1)S(1)} %get-tuple-element.12.cols, bf16[8,512,256]{2,1,0:T(8,128)(2,1)S(1)} %get-tuple-element.13.rows), custom_call_target="tpu_custom_call" | custom-call | flops 2147483648 | bytes 8388608 | tf_op jit(solution)/shard_map/facet_blocks/pallas_call | solution.py:178
  22.0 0.1 collective-permute-start.6
  22.1 0.1 pad_add_fusion.place
  22.1 1.4 %col_table.1.table = bf16[8,512,128]{2,1,0:T(8,128)(2,1)S(1)} custom-call(s32[2]{0:T(128)S(1)} %pad_add_fusion.place, bf16[128,512]{1,0:T(8,128)(2,1)S(1)} %facet_blocks.4.after.refs_3_), custom_call_target="tpu_custom_call" | custom-call | flops 4194304 | bytes 1048576 | tf_op jit(solution)/shard_map/col_table/pallas_call | solution.py:401
  23.5 0.0 collective-permute-done.refs_0_
  23.5 0.0 collective-permute-done.1.refs_1_
  23.5 0.6 collective-permute-start.3
  24.1 0.5 collective-permute-done.2.refs_2_
  24.5 0.0 collective-permute-start.5
  24.5 0.5 collective-permute-start.4
  25.1 0.0 copy-done
  25.1 0.0 copy-done.1
  25.1 0.0 copy-done.2
  25.1 0.0 collective-permute-done.6.refs_7_
  25.1 0.8 %collective-permute-done.5.refs_6_ = bf16[128,512]{1,0:T(8,128)(2,1)S(1)} collective-permute-done((bf16[128,512]{1,0:T(8,128)(2,1)S(1)}, bf16[128,512]{1,0:T(8,128)(2,1)S(1)}, u32[]{:S(2)}, u32[]{:S(2)}) %collective-permute-start.5) | collective-permute-done | bytes 131104 | tf_op jit(solution)/shard_map/ppermute | solution.py:419
  25.9 0.0 collective-permute-done.3.refs_4_
  25.9 0.2 collective-permute-done.4.refs_5_
  26.1 0.7 %column_sums.1.after.refs_0_ = bf16[512,256]{1,0:T(8,128)(2,1)S(1)} custom-call(bf16[8,512,128]{2,1,0:T(8,128)(2,1)S(1)} %col_table.1.table, bf16[128,512]{1,0:T(8,128)(2,1)S(1)} %collective-permute-done.refs_0_, bf16[128,512]{1,0:T(8,128)(2,1)S(1)} %collective-permute-done.1.refs_1_, bf16[128,512]{1,0:T(8,128)(2,1)S(1)} %collective-permute-done.2.refs_2_, ...), custom_call_target="tpu_custom_call" | custom-call | flops 536870912 | bytes 2097152 | tf_op jit(solution)/shard_map/column_sums/pallas_call | solution.py:252
  26.8 3.1 %collective-permute-start.12 = (bf16[8,4608]{1,0:T(8,128)(2,1)S(1)}, bf16[8,4608]{1,0:T(8,128)(2,1)S(1)}, u32[]{:S(2)}, u32[]{:S(2)}) collective-permute-start(bf16[8,4608]{1,0:T(8,128)(2,1)S(1)} %query.1), channel_id=1, source_target_pairs={{0,6},{1,7},{2,4},{3,5},{4,2},{5,3},{6,0},{7,1},{8,14},{9,15},{10,... | collective-permute-start | bytes 221192 | tf_op jit(solution)/shard_map/ppermute | solution.py:440
  29.9 0.0 collective-permute-start.11
  29.9 1.3 %collective-permute-start.10 = (bf16[8,4608]{1,0:T(8,128)(2,1)S(1)}, bf16[8,4608]{1,0:T(8,128)(2,1)S(1)}, u32[]{:S(2)}, u32[]{:S(2)}) collective-permute-start(bf16[8,4608]{1,0:T(8,128)(2,1)S(1)} %query.1), channel_id=1, source_target_pairs={{0,2},{1,3},{2,0},{3,1},{4,6},{5,7},{6,4},{7,5},{8,10},{9,11},{10,... | collective-permute-start | bytes 221192 | tf_op jit(solution)/shard_map/ppermute | solution.py:440
  31.2 1.5 %collective-permute-start.8 = (bf16[512,256]{1,0:T(8,128)(2,1)S(1)}, bf16[512,256]{1,0:T(8,128)(2,1)S(1)}, u32[]{:S(2)}, u32[]{:S(2)}) collective-permute-start(bf16[512,256]{1,0:T(8,128)(2,1)S(1)} %column_sums.1.after.refs_0_), channel_id=1, source_target_pairs={{0,16},{8,24},{16,0},{24,8},{1,17},{9,25},{17,1},{25,9},{2,18},{10... | collective-permute-start | bytes 786440 | tf_op jit(solution)/shard_map/ppermute | solution.py:423
  32.8 1.5 %collective-permute-start.7 = (bf16[512,256]{1,0:T(8,128)(2,1)S(1)}, bf16[512,256]{1,0:T(8,128)(2,1)S(1)}, u32[]{:S(2)}, u32[]{:S(2)}) collective-permute-start(bf16[512,256]{1,0:T(8,128)(2,1)S(1)} %column_sums.1.after.refs_0_), channel_id=1, source_target_pairs={{0,8},{8,0},{16,24},{24,16},{1,9},{9,1},{17,25},{25,17},{2,10},{10... | collective-permute-start | bytes 786440 | tf_op jit(solution)/shard_map/ppermute | solution.py:423
  34.3 0.0 collective-permute-done.12
  34.3 2.6 %collective-permute-done.11 = bf16[8,4608]{1,0:T(8,128)(2,1)S(1)} collective-permute-done((bf16[8,4608]{1,0:T(8,128)(2,1)S(1)}, bf16[8,4608]{1,0:T(8,128)(2,1)S(1)}, u32[]{:S(2)}, u32[]{:S(2)}) %collective-permute-start.11) | collective-permute-done | bytes 73760 | tf_op jit(solution)/shard_map/ppermute | solution.py:440
  36.8 0.0 collective-permute-done.10
  36.9 0.1 collective-permute-start.13
  37.0 2.5 %collective-permute-start.9 = (bf16[512,256]{1,0:T(8,128)(2,1)S(1)}, bf16[512,256]{1,0:T(8,128)(2,1)S(1)}, u32[]{:S(2)}, u32[]{:S(2)}) collective-permute-start(bf16[512,256]{1,0:T(8,128)(2,1)S(1)} %column_sums.1.after.refs_0_), channel_id=1, source_target_pairs={{0,24},{8,16},{16,8},{24,0},{1,25},{9,17},{17,9},{25,1},{2,26},{10... | collective-permute-start | bytes 786440 | tf_op jit(solution)/shard_map/ppermute | solution.py:423
  39.5 2.4 %row_table.1.table = bf16[8,128,1024]{2,1,0:T(8,128)(2,1)S(1)} custom-call(s32[2]{0:T(128)S(1)} %pad_add_fusion.place, bf16[512,256]{1,0:T(8,128)(2,1)S(1)} %column_sums.1.after.refs_0_), custom_call_target="tpu_custom_call" | custom-call | flops 8388608 | bytes 2097152 | tf_op jit(solution)/shard_map/row_table/pallas_call | solution.py:424
  41.9 0.0 copy-start.3
  41.9 0.0 collective-permute-done.8.refs_2_
  41.9 0.0 collective-permute-done.7.refs_1_
  41.9 1.0 %partial_rows.1.partial = f32[512,1024]{1,0:T(8,128)S(1)} custom-call(bf16[8,128,1024]{2,1,0:T(8,128)(2,1)S(1)} %row_table.1.table, bf16[512,256]{1,0:T(8,128)(2,1)S(1)} %column_sums.1.after.refs_0_, bf16[512,256]{1,0:T(8,128)(2,1)S(1)} %collective-permute-done.7.refs_1_, bf16[512,256]{1,0:T(8,128)(2,1)S(1)} %collective-permute-done.8.refs_2_), custom_call_target="tpu_custom_call" | custom-call | flops 1073741824 | bytes 4194304 | tf_op jit(solution)/shard_map/partial_rows/pallas_call | solution.py:443
  42.9 3.7 %collective-permute-done.9.last = bf16[512,256]{1,0:T(8,128)(2,1)S(1)} collective-permute-done((bf16[512,256]{1,0:T(8,128)(2,1)S(1)}, bf16[512,256]{1,0:T(8,128)(2,1)S(1)}, u32[]{:S(2)}, u32[]{:S(2)}) %collective-permute-start.9) | collective-permute-done | bytes 262176 | tf_op jit(solution)/shard_map/ppermute | solution.py:423
  46.6 0.0 collective-permute-done.13.queries_other
  46.6 0.0 copy-done.3
  46.6 7.9 %degrid.1 = (f32[4,2,2048]{2,1,0:T(2,128)S(1)}, f32[4,2,2048]{2,1,0:T(2,128)S(1)}) custom-call(s32[2]{0:T(128)S(1)} %pad_add_fusion.place, s32[32]{0:T(128)S(1)} %copy-done.3, bf16[8,128,1024]{2,1,0:T(8,128)(2,1)S(1)} %row_table.1.table, f32[512,1024]{1,0:T(8,128)S(1)} %partial_rows.1.partial, bf16[512,256]{1,0:T(8,128)(2,1)S(1)} %collective-permute-done.9.last, ...), custom_call_target="tpu_custom_call" | custom-call | flops 8589934592 | bytes 4194304 | tf_op jit(solution)/shard_map/degrid/pallas_call | solution.py:353
  54.5 0.1 collective-permute-start.14
  54.5 1.2 %collective-permute-done.14 = f32[4,2,2048]{2,1,0:T(2,128)S(1)} collective-permute-done((f32[4,2,2048]{2,1,0:T(2,128)S(1)}, f32[4,2,2048]{2,1,0:T(2,128)S(1)}, u32[]{:S(2)}, u32[]{:S(2)}) %collective-permute-start.14) | collective-permute-done | bytes 65568 | tf_op jit(solution)/shard_map/ppermute | solution.py:458
  55.8 0.1 collective-permute-start.15
  55.9 0.1 collective-permute-start.17
  56.0 3.4 %collective-permute-start.16 = (f32[2,2048]{1,0:T(2,128)S(1)}, f32[2,2048]{1,0:T(2,128)S(1)}, u32[]{:S(2)}, u32[]{:S(2)}) collective-permute-start(f32[2,2048]{1,0:T(2,128)S(1)} %get-tuple-element.21), channel_id=1, source_target_pairs={{0,4},{1,5},{2,6},{3,7},{4,0},{5,1},{6,2},{7,3},{8,12},{9,13},{10,... | collective-permute-start | bytes 49160 | tf_op jit(solution)/shard_map/ppermute | solution.py:462
  59.4 0.2 collective-permute-done.15
  59.6 1.9 %collective-permute-done.17 = f32[2,2048]{1,0:T(2,128)S(1)} collective-permute-done((f32[2,2048]{1,0:T(2,128)S(1)}, f32[2,2048]{1,0:T(2,128)S(1)}, u32[]{:S(2)}, u32[]{:S(2)}) %collective-permute-start.17) | collective-permute-done | bytes 16416 | tf_op jit(solution)/shard_map/ppermute | solution.py:462
  61.5 0.0 collective-permute-done.16
  61.5 0.6 %fusion.2 = f32[2,2048]{1,0:T(2,128)} fusion(f32[2,2048]{1,0:T(2,128)S(1)} %collective-permute-done.17, f32[2,2048]{1,0:T(2,128)S(1)} %collective-permute-done.16, f32[2,2048]{1,0:T(2,128)S(1)} %collective-permute-done.15, f32[4,2,2048]{2,1,0:T(2,128)S(1)} %add.12), kind=kLoop, calls=%fused_computation.7 | loop fusion | flops 12288 | bytes 81920 | tf_op jit(solution)/shard_map/add | solution.py:462
  (5 shorter events, 0.1 us)
Async XLA Ops:
  0.8 4.5 %slice-start = ((s8[8388608]{0:T(1024)(128)(4,1)}), s8[4194304]{0:T(1024)(128)(4,1)S(1)}, s32[]{:S(2)}) async-start(s8[8388608]{0:T(1024)(128)(4,1)} %bitcast.20), calls=%async_computation | async-start | bytes 8388608
  0.8 4.4 %slice-start.1 = ((s8[8388608]{0:T(1024)(128)(4,1)}), s8[4194304]{0:T(1024)(128)(4,1)S(1)}, s32[]{:S(2)}) async-start(s8[8388608]{0:T(1024)(128)(4,1)} %bitcast.20), calls=%async_computation.1 | async-start | bytes 8388608
  8.0 15.5 %collective-permute-start = (bf16[128,512]{1,0:T(8,128)(2,1)S(1)}, bf16[128,512]{1,0:T(8,128)(2,1)S(1)}, u32[]{:S(2)}, u32[]{:S(2)}) collective-permute-start(bf16[128,512]{1,0:T(8,128)(2,1)S(1)} %facet_blocks.5), channel_id=1, source_target_pairs={{0,4},{1,5},{2,6},{3,7},{4,0},{5,1},{6,2},{7,3},{8,12},{9,13},{10,... | collective-permute-start | bytes 393224 | tf_op jit(solution)/shard_map/ppermute | solution.py:398
  14.8 8.7 %collective-permute-start.1 = (bf16[128,512]{1,0:T(8,128)(2,1)S(1)}, bf16[128,512]{1,0:T(8,128)(2,1)S(1)}, u32[]{:S(2)}, u32[]{:S(2)}) collective-permute-start(bf16[128,512]{1,0:T(8,128)(2,1)S(1)} %facet_blocks.6), channel_id=1, source_target_pairs={{0,6},{1,7},{2,4},{3,5},{4,2},{5,3},{6,0},{7,1},{8,14},{9,15},{10,... | collective-permute-start | bytes 393224 | tf_op jit(solution)/shard_map/ppermute | solution.py:398
  18.9 6.1 %copy-start = (f32[8,2048]{1,0:T(8,128)S(1)}, f32[8,2048]{1,0:T(8,128)}, u32[]{:S(2)}) copy-start(f32[8,2048]{1,0:T(8,128)} %col_kernel.1) | copy-start | bytes 196612
  18.9 6.1 %copy-start.1 = (bf16[8,2048]{1,0:T(8,128)(2,1)S(1)}, bf16[8,2048]{1,0:T(8,128)(2,1)}, u32[]{:S(2)}) copy-start(bf16[8,2048]{1,0:T(8,128)(2,1)} %row_kernel.1) | copy-start | bytes 98308
  18.9 6.1 %copy-start.2 = (s32[2,2048]{1,0:T(2,128)S(1)}, s32[2,2048]{1,0:T(2,128)}, u32[]{:S(2)}) copy-start(s32[2,2048]{1,0:T(2,128)} %vis_cells.1) | copy-start | bytes 49156
  19.0 5.6 %collective-permute-start.2 = (bf16[128,512]{1,0:T(8,128)(2,1)S(1)}, bf16[128,512]{1,0:T(8,128)(2,1)S(1)}, u32[]{:S(2)}, u32[]{:S(2)}) collective-permute-start(bf16[128,512]{1,0:T(8,128)(2,1)S(1)} %facet_blocks.7), channel_id=1, source_target_pairs={{0,2},{1,3},{2,0},{3,1},{4,6},{5,7},{6,4},{7,5},{8,10},{9,11},{10,... | collective-permute-start | bytes 393224 | tf_op jit(solution)/shard_map/ppermute | solution.py:398
  22.0 3.1 %collective-permute-start.6 = (bf16[128,512]{1,0:T(8,128)(2,1)S(1)}, bf16[128,512]{1,0:T(8,128)(2,1)S(1)}, u32[]{:S(2)}, u32[]{:S(2)}) collective-permute-start(bf16[128,512]{1,0:T(8,128)(2,1)S(1)} %facet_blocks.4.after.refs_3_), channel_id=1, source_target_pairs={{0,1},{1,0},{2,3},{3,2},{4,5},{5,4},{6,7},{7,6},{8,9},{9,8},{10,11... | collective-permute-start | bytes 393224 | tf_op jit(solution)/shard_map/ppermute | solution.py:419
  23.5 2.4 %collective-permute-start.3 = (bf16[128,512]{1,0:T(8,128)(2,1)S(1)}, bf16[128,512]{1,0:T(8,128)(2,1)S(1)}, u32[]{:S(2)}, u32[]{:S(2)}) collective-permute-start(bf16[128,512]{1,0:T(8,128)(2,1)S(1)} %collective-permute-done.refs_0_), channel_id=1, source_target_pairs={{0,1},{1,0},{2,3},{3,2},{4,5},{5,4},{6,7},{7,6},{8,9},{9,8},{10,11... | collective-permute-start | bytes 393224 | tf_op jit(solution)/shard_map/ppermute | solution.py:419
  24.5 1.3 %collective-permute-start.5 = (bf16[128,512]{1,0:T(8,128)(2,1)S(1)}, bf16[128,512]{1,0:T(8,128)(2,1)S(1)}, u32[]{:S(2)}, u32[]{:S(2)}) collective-permute-start(bf16[128,512]{1,0:T(8,128)(2,1)S(1)} %collective-permute-done.2.refs_2_), channel_id=1, source_target_pairs={{0,1},{1,0},{2,3},{3,2},{4,5},{5,4},{6,7},{7,6},{8,9},{9,8},{10,11... | collective-permute-start | bytes 393224 | tf_op jit(solution)/shard_map/ppermute | solution.py:419
  24.5 1.5 %collective-permute-start.4 = (bf16[128,512]{1,0:T(8,128)(2,1)S(1)}, bf16[128,512]{1,0:T(8,128)(2,1)S(1)}, u32[]{:S(2)}, u32[]{:S(2)}) collective-permute-start(bf16[128,512]{1,0:T(8,128)(2,1)S(1)} %collective-permute-done.1.refs_1_), channel_id=1, source_target_pairs={{0,1},{1,0},{2,3},{3,2},{4,5},{5,4},{6,7},{7,6},{8,9},{9,8},{10,11... | collective-permute-start | bytes 393224 | tf_op jit(solution)/shard_map/ppermute | solution.py:419
  26.8 7.5 %collective-permute-start.12 = (bf16[8,4608]{1,0:T(8,128)(2,1)S(1)}, bf16[8,4608]{1,0:T(8,128)(2,1)S(1)}, u32[]{:S(2)}, u32[]{:S(2)}) collective-permute-start(bf16[8,4608]{1,0:T(8,128)(2,1)S(1)} %query.1), channel_id=1, source_target_pairs={{0,6},{1,7},{2,4},{3,5},{4,2},{5,3},{6,0},{7,1},{8,14},{9,15},{10,... | collective-permute-start | bytes 221192 | tf_op jit(solution)/shard_map/ppermute | solution.py:440
  29.9 6.9 %collective-permute-start.11 = (bf16[8,4608]{1,0:T(8,128)(2,1)S(1)}, bf16[8,4608]{1,0:T(8,128)(2,1)S(1)}, u32[]{:S(2)}, u32[]{:S(2)}) collective-permute-start(bf16[8,4608]{1,0:T(8,128)(2,1)S(1)} %query.1), channel_id=1, source_target_pairs={{0,4},{1,5},{2,6},{3,7},{4,0},{5,1},{6,2},{7,3},{8,12},{9,13},{10,... | collective-permute-start | bytes 221192 | tf_op jit(solution)/shard_map/ppermute | solution.py:440
  29.9 6.9 %collective-permute-start.10 = (bf16[8,4608]{1,0:T(8,128)(2,1)S(1)}, bf16[8,4608]{1,0:T(8,128)(2,1)S(1)}, u32[]{:S(2)}, u32[]{:S(2)}) collective-permute-start(bf16[8,4608]{1,0:T(8,128)(2,1)S(1)} %query.1), channel_id=1, source_target_pairs={{0,2},{1,3},{2,0},{3,1},{4,6},{5,7},{6,4},{7,5},{8,10},{9,11},{10,... | collective-permute-start | bytes 221192 | tf_op jit(solution)/shard_map/ppermute | solution.py:440
  31.2 10.6 %collective-permute-start.8 = (bf16[512,256]{1,0:T(8,128)(2,1)S(1)}, bf16[512,256]{1,0:T(8,128)(2,1)S(1)}, u32[]{:S(2)}, u32[]{:S(2)}) collective-permute-start(bf16[512,256]{1,0:T(8,128)(2,1)S(1)} %column_sums.1.after.refs_0_), channel_id=1, source_target_pairs={{0,16},{8,24},{16,0},{24,8},{1,17},{9,25},{17,1},{25,9},{2,18},{10... | collective-permute-start | bytes 786440 | tf_op jit(solution)/shard_map/ppermute | solution.py:423
  32.8 9.1 %collective-permute-start.7 = (bf16[512,256]{1,0:T(8,128)(2,1)S(1)}, bf16[512,256]{1,0:T(8,128)(2,1)S(1)}, u32[]{:S(2)}, u32[]{:S(2)}) collective-permute-start(bf16[512,256]{1,0:T(8,128)(2,1)S(1)} %column_sums.1.after.refs_0_), channel_id=1, source_target_pairs={{0,8},{8,0},{16,24},{24,16},{1,9},{9,1},{17,25},{25,17},{2,10},{10... | collective-permute-start | bytes 786440 | tf_op jit(solution)/shard_map/ppermute | solution.py:423
  36.9 9.7 %collective-permute-start.13 = (bf16[4,8,4608]{2,1,0:T(8,128)(2,1)S(1)}, bf16[4,8,4608]{2,1,0:T(8,128)(2,1)S(1)}, u32[]{:S(2)}, u32[]{:S(2)}) collective-permute-start(bf16[4,8,4608]{2,1,0:T(8,128)(2,1)S(1)} %pad_maximum_fusion.queries_own), channel_id=1, source_target_pairs={{0,1},{1,0},{2,3},{3,2},{4,5},{5,4},{6,7},{7,6},{8,9},{9,8},{10,11... | collective-permute-start | bytes 884744 | tf_op jit(solution)/shard_map/ppermute | solution.py:442
  37.0 9.6 %collective-permute-start.9 = (bf16[512,256]{1,0:T(8,128)(2,1)S(1)}, bf16[512,256]{1,0:T(8,128)(2,1)S(1)}, u32[]{:S(2)}, u32[]{:S(2)}) collective-permute-start(bf16[512,256]{1,0:T(8,128)(2,1)S(1)} %column_sums.1.after.refs_0_), channel_id=1, source_target_pairs={{0,24},{8,16},{16,8},{24,0},{1,25},{9,17},{17,9},{25,1},{2,26},{10... | collective-permute-start | bytes 786440 | tf_op jit(solution)/shard_map/ppermute | solution.py:423
  41.9 4.7 %copy-start.3 = (s32[32]{0:T(128)S(1)}, s32[32]{0:T(128)}, u32[]{:S(2)}) copy-start(s32[32]{0:T(128)} %readers.1) | copy-start | bytes 388
  54.5 1.3 %collective-permute-start.14 = (f32[4,2,2048]{2,1,0:T(2,128)S(1)}, f32[4,2,2048]{2,1,0:T(2,128)S(1)}, u32[]{:S(2)}, u32[]{:S(2)}) collective-permute-start(f32[4,2,2048]{2,1,0:T(2,128)S(1)} %get-tuple-element.18), channel_id=1, source_target_pairs={{0,1},{1,0},{2,3},{3,2},{4,5},{5,4},{6,7},{7,6},{8,9},{9,8},{10,11... | collective-permute-start | bytes 196616 | tf_op jit(solution)/shard_map/ppermute | solution.py:458
  55.8 3.8 %collective-permute-start.15 = (f32[2,2048]{1,0:T(2,128)S(1)}, f32[2,2048]{1,0:T(2,128)S(1)}, u32[]{:S(2)}, u32[]{:S(2)}) collective-permute-start(f32[2,2048]{1,0:T(2,128)S(1)} %get-tuple-element.19), channel_id=1, source_target_pairs={{0,2},{1,3},{2,0},{3,1},{4,6},{5,7},{6,4},{7,5},{8,10},{9,11},{10,... | collective-permute-start | bytes 49160 | tf_op jit(solution)/shard_map/ppermute | solution.py:462
  55.9 5.6 %collective-permute-start.17 = (f32[2,2048]{1,0:T(2,128)S(1)}, f32[2,2048]{1,0:T(2,128)S(1)}, u32[]{:S(2)}, u32[]{:S(2)}) collective-permute-start(f32[2,2048]{1,0:T(2,128)S(1)} %get-tuple-element.20), channel_id=1, source_target_pairs={{0,6},{1,7},{2,4},{3,5},{4,2},{5,3},{6,0},{7,1},{8,14},{9,15},{10,... | collective-permute-start | bytes 49160 | tf_op jit(solution)/shard_map/ppermute | solution.py:462
  56.0 5.5 %collective-permute-start.16 = (f32[2,2048]{1,0:T(2,128)S(1)}, f32[2,2048]{1,0:T(2,128)S(1)}, u32[]{:S(2)}, u32[]{:S(2)}) collective-permute-start(f32[2,2048]{1,0:T(2,128)S(1)} %get-tuple-element.21), channel_id=1, source_target_pairs={{0,4},{1,5},{2,6},{3,7},{4,0},{5,1},{6,2},{7,3},{8,12},{9,13},{10,... | collective-permute-start | bytes 49160 | tf_op jit(solution)/shard_map/ppermute | solution.py:462
